TPU v7x, 256 devices: a whole 4x4x8 slice. The times are simulated.
256 devices in a mesh: section: 4 (over x), dp: 2 (over core), expert: 32 (over z, y).
Axes of the slice: x: 4, y: 4, z: 8, core: 2. Of those that a mesh axis runs over, the one named last changes fastest.
Arguments:
- tokens: bfloat16 [4, 8192, 2048], P('section', ('dp', 'expert')), may hold values from -6 to 6
- out_grad: bfloat16 [4, 8192, 2048], P('section', ('dp', 'expert')), may hold values from -6 to 6
- expert_ids: int32 [4, 8192, 2], P('section', ('dp', 'expert')), may hold values from 0 to 31, all different within a row; in each aligned block of 128 rows (0 to 127, 128 to 255, ..., all dimensions but the last counted through in order) at most 16 rows name the same one
- route_probs: float32 [4, 8192, 2], P('section', ('dp', 'expert')), may hold values from 0.1 to 1
- gate_weight: bfloat16 [4, 32, 2048, 768], P('section', 'expert', None, 'dp'), may hold values from -0.125 to 0.125
- up_weight: bfloat16 [4, 32, 2048, 768], P('section', 'expert', None, 'dp'), may hold values from -0.125 to 0.125
- down_weight: bfloat16 [4, 32, 768, 2048], P('section', 'expert', 'dp'), may hold values from -0.21875 to 0.21875
Outputs:
- grad_in: bfloat16 [4, 8192, 2048], P('section', ('dp', 'expert'))
- prob_grad: float32 [4, 8192, 2], P('section', ('dp', 'expert'))
- gate_weight_grad: bfloat16 [4, 32, 2048, 768], P('section', 'expert', None, 'dp')
- up_weight_grad: bfloat16 [4, 32, 2048, 768], P('section', 'expert', None, 'dp')
- down_weight_grad: bfloat16 [4, 32, 768, 2048], P('section', 'expert', 'dp')
Inputs may be any that keep to these rules, and one draw needn't show every extreme that they name: `expert_ids`: each token names 2 different experts; among the 128 tokens of one device (aligned blocks of 128 tokens of a section) no expert is named more than 16 times, a bound that some block reaches.
All inputs are finite; a program needn't handle non-finite values.
Results may differ from a plain program's by a relative error of at most 0.023.
Values may be sent and summed in bfloat16 or wider, within the bound.
A program may use at most 128 MiB of HBM per device.

v0:
```python
import jax
import jax.numpy as jnp
from jax import lax
from jax.sharding import PartitionSpec as P


def from_behind(shard, axis, by):
    length = lax.axis_size(axis)
    return lax.ppermute(shard, axis, [(i, (i + by) % length) for i in range(length)])


def expert_grads(rows_in, grads_in, weights_in, gate_part, up_part, down_part):
    contract_last = (((1,), (1,)), ((), ()))
    contract_first = (((0,), (0,)), ((), ()))
    gate_pre = jnp.dot(rows_in, gate_part, preferred_element_type=jnp.float32)
    up_pre = jnp.dot(rows_in, up_part, preferred_element_type=jnp.float32)
    sigmoid_gate = jax.nn.sigmoid(gate_pre)
    activated = gate_pre * sigmoid_gate * up_pre
    scaled_act = (weights_in[:, None] * activated).astype(jnp.bfloat16)
    hidden_grad = lax.dot_general(
        grads_in, down_part, contract_last, preferred_element_type=jnp.float32
    )
    prob_part = jnp.sum(activated * hidden_grad, axis=1)
    hidden_scaled = weights_in[:, None] * hidden_grad
    gate_grad = (
        hidden_scaled * up_pre * sigmoid_gate * (1.0 + gate_pre * (1.0 - sigmoid_gate))
    ).astype(jnp.bfloat16)
    up_grad = (hidden_scaled * gate_pre * sigmoid_gate).astype(jnp.bfloat16)
    route_dx = lax.dot_general(
        gate_grad, gate_part, contract_last, preferred_element_type=jnp.float32
    ) + lax.dot_general(up_grad, up_part, contract_last, preferred_element_type=jnp.float32)
    grad_gate = lax.dot_general(
        rows_in, gate_grad, contract_first, preferred_element_type=jnp.float32
    )
    grad_up = lax.dot_general(rows_in, up_grad, contract_first, preferred_element_type=jnp.float32)
    grad_down = lax.dot_general(
        scaled_act, grads_in, contract_first, preferred_element_type=jnp.float32
    )
    return (route_dx, prob_part, grad_gate, grad_up, grad_down)


def per_device(tokens, out_grad, expert_ids, route_probs, gate_weight, up_weight, down_weight):
    local_tokens = tokens[0]
    local_grads = out_grad[0]
    tok_count, row_width = local_tokens.shape
    top_count = expert_ids.shape[2]
    groups = lax.axis_size("expert")
    capacity = 2 * tok_count * top_count // groups
    slots_all = groups * capacity
    route_ids = expert_ids[0].reshape(-1)
    hit_table = (route_ids[:, None] == jnp.arange(groups, dtype=jnp.int32)[None, :]).astype(
        jnp.int32
    )
    before = jnp.cumsum(hit_table, axis=0) - hit_table
    slot_rank = jnp.sum(before * hit_table, axis=1)
    slot_of = route_ids * capacity + slot_rank
    placed = slot_of[None, :] == jnp.arange(slots_all, dtype=jnp.int32)[:, None]
    per_token = jnp.any(placed.reshape(slots_all, tok_count, top_count), axis=2).astype(
        jnp.bfloat16
    )
    send_rows = jnp.dot(per_token, local_tokens, preferred_element_type=jnp.float32).astype(
        jnp.bfloat16
    )
    send_grads = jnp.dot(per_token, local_grads, preferred_element_type=jnp.float32).astype(
        jnp.bfloat16
    )
    probs_flat = route_probs[0].reshape(-1)
    send_probs = jnp.sum(jnp.where(placed, probs_flat[None, :], 0.0), axis=1)
    recv_rows, recv_grads, recv_probs = (
        lax.all_to_all(
            send_rows.reshape(groups, capacity, row_width),
            "expert",
            split_axis=0,
            concat_axis=0,
            tiled=True,
        ),
        lax.all_to_all(
            send_grads.reshape(groups, capacity, row_width),
            "expert",
            split_axis=0,
            concat_axis=0,
            tiled=True,
        ),
        lax.all_to_all(
            send_probs.reshape(groups, capacity).astype(jnp.bfloat16),
            "expert",
            split_axis=0,
            concat_axis=0,
            tiled=True,
        ).astype(jnp.float32),
    )
    recv_rows = recv_rows.reshape(slots_all, row_width)
    recv_grads = recv_grads.reshape(slots_all, row_width)
    recv_probs = recv_probs.reshape(slots_all)
    gate_part = gate_weight[0, 0]
    up_part = up_weight[0, 0]
    down_part = down_weight[0, 0]
    gate_full, up_full, down_full = (
        lax.all_gather(gate_part, "dp", axis=1, tiled=True),
        lax.all_gather(up_part, "dp", axis=1, tiled=True),
        lax.all_gather(down_part, "dp", axis=0, tiled=True),
    )
    route_dx, prob_part, grad_gate, grad_up, grad_down = expert_grads(
        recv_rows, recv_grads, recv_probs, gate_full, up_full, down_full
    )
    grad_gate, grad_up, grad_down = (
        lax.psum_scatter(
            grad_gate.astype(jnp.bfloat16), "dp", scatter_dimension=1, tiled=True
        ).astype(jnp.float32),
        lax.psum_scatter(
            grad_up.astype(jnp.bfloat16), "dp", scatter_dimension=1, tiled=True
        ).astype(jnp.float32),
        lax.psum_scatter(
            grad_down.astype(jnp.bfloat16), "dp", scatter_dimension=0, tiled=True
        ).astype(jnp.float32),
    )
    back_rows, back_probs = (
        lax.all_to_all(
            route_dx.astype(jnp.bfloat16).reshape(groups, capacity, row_width),
            "expert",
            split_axis=0,
            concat_axis=0,
            tiled=True,
        ),
        lax.all_to_all(
            prob_part.reshape(groups, capacity).astype(jnp.bfloat16),
            "expert",
            split_axis=0,
            concat_axis=0,
            tiled=True,
        ).astype(jnp.float32),
    )
    token_grad = lax.dot_general(
        per_token,
        back_rows.reshape(slots_all, row_width),
        (((0,), (0,)), ((), ())),
        preferred_element_type=jnp.float32,
    ).astype(jnp.bfloat16)
    route_grad = jnp.sum(jnp.where(placed, back_probs.reshape(slots_all)[:, None], 0.0), axis=0)
    route_grad = route_grad.reshape(tok_count, top_count)
    upstream = from_behind(token_grad, "section", -1)
    return (
        upstream[None],
        route_grad[None],
        grad_gate.astype(jnp.bfloat16)[None, None],
        grad_up.astype(jnp.bfloat16)[None, None],
        grad_down.astype(jnp.bfloat16)[None, None],
    )


def solution(mesh):
    in_specs = (
        P("section", ("dp", "expert"), None),
        P("section", ("dp", "expert"), None),
        P("section", ("dp", "expert"), None),
        P("section", ("dp", "expert"), None),
        P("section", "expert", None, "dp"),
        P("section", "expert", None, "dp"),
        P("section", "expert", "dp", None),
    )
    out_specs = (
        P("section", ("dp", "expert"), None),
        P("section", ("dp", "expert"), None),
        P("section", "expert", None, "dp"),
        P("section", "expert", None, "dp"),
        P("section", "expert", "dp", None),
    )
    return jax.shard_map(
        per_device, mesh=mesh, in_specs=in_specs, out_specs=out_specs, check_vma=False
    )
```

profile of v0, /device:TPU:2, one launch (start us, length us, event | category | flops | bytes accessed | tf_op | source)
XLA Modules:
  0.0 273.3 jit_solution(8630525464374877536)
XLA Ops:
  7.2 0.0 all-gather.11.cloned.1.call-start
  7.2 0.7 all-gather.11.cloned.1.call-update
  7.9 0.8 copy.27
  8.7 0.1 eq.49
  8.8 0.1 eq.45
  9.0 0.6 reduce-window.6
  9.6 0.2 slice_reduce_fusion
  9.8 0.1 fusion.18
  9.9 0.1 reduce_sum.39
  10.1 0.1 copy.31
  10.2 0.1 fusion.15
  10.2 2.0 convolution_convert_fusion.3
  12.3 11.6 %all-to-all-start.2 = ((bf16[32,16,2048]{2,1,0:T(8,128)(2,1)}), bf16[32,16,2048]{2,1,0:T(8,128)(2,1)S(1)}, u32[]{:S(2)}, u32[]{:S(2)}) async-start(bf16[32,16,2048]{2,1,0:T(8,128)(2,1)} %bitcast.7), calls=%async_computation.2 | async-start | bytes 4194304 | tf_op jit(solution)/shard_map/all_to_all | solution.py:70
  23.9 0.0 all-gather.9.cloned.1.call-start
  24.0 0.7 all-gather.9.cloned.1.call-update
  24.7 2.0 convolution_convert_fusion.4
  26.7 47.4 %all-to-all-done.2 = bf16[32,16,2048]{2,1,0:T(8,128)(2,1)S(1)} async-done(((bf16[32,16,2048]{2,1,0:T(8,128)(2,1)}), bf16[32,16,2048]{2,1,0:T(8,128)(2,1)S(1)}, u32[]{:S(2)}, u32[]{:S(2)}) %all-to-all-start.2) | async-done | bytes 2097184 | tf_op jit(solution)/shard_map/all_to_all | solution.py:70
  74.1 6.1 %all-to-all-start.1 = ((bf16[32,16,2048]{2,1,0:T(8,128)(2,1)}), bf16[32,16,2048]{2,1,0:T(8,128)(2,1)}, u32[]{:S(2)}, u32[]{:S(2)}) async-start(bf16[32,16,2048]{2,1,0:T(8,128)(2,1)} %bitcast.3), calls=%async_computation.1 | async-start | bytes 4194304 | tf_op jit(solution)/shard_map/all_to_all | solution.py:77
  80.2 0.0 all-gather.7.cloned.1.call-start
  80.2 0.7 all-gather.7.cloned.1.call-update
  80.9 0.0 all-gather.11.cloned.1.call-done
  80.9 4.8 %fusion.2 = f32[512,768]{1,0:T(8,128)} fusion(bf16[512,2048]{1,0:T(8,128)(2,1)S(1)} %bitcast.75, bf16[1,1,2048,768]{3,2,1,0:T(8,128)(2,1)} %all-gather.11.cloned.1.call-done), kind=kOutput, calls=%fused_computation.6 | convolution fusion | flops 1610612736 | bytes 6815744 | tf_op jit(solution)/shard_map/dot_general | solution.py:15
  85.7 4.8 %fusion.6 = f32[512,768]{1,0:T(8,128)} fusion(bf16[512,2048]{1,0:T(8,128)(2,1)S(1)} %bitcast.76, bf16[1,1,2048,768]{3,2,1,0:T(8,128)(2,1)} %all-gather.9.cloned.1.call-done), kind=kOutput, calls=%fused_computation.10 | convolution fusion | flops 1610612736 | bytes 6815744 | tf_op jit(solution)/shard_map/dot_general | solution.py:16
  90.6 10.9 %all-gather.7.cloned.1.call-done = bf16[1,1,768,2048]{3,2,1,0:T(8,128)(2,1)} async-done(((bf16[1,1,384,2048]{3,2,1,0:T(8,128)(2,1)}), bf16[1,1,768,2048]{3,2,1,0:T(8,128)(2,1)}) %all-gather.7.cloned.1.call-update) | async-done | bytes 3145744 | tf_op jit(solution)/shard_map/all_gather | solution.py:101
  101.5 27.8 %all-to-all-done.1 = bf16[32,16,2048]{2,1,0:T(8,128)(2,1)} async-done(((bf16[32,16,2048]{2,1,0:T(8,128)(2,1)}), bf16[32,16,2048]{2,1,0:T(8,128)(2,1)}, u32[]{:S(2)}, u32[]{:S(2)}) %all-to-all-start.1) | async-done | bytes 2097184 | tf_op jit(solution)/shard_map/all_to_all | solution.py:77
  129.3 6.5 %multiply_reduce_fusion = (bf16[512]{0:T(512)(128)(2,1)S(1)}, f32[512,768]{1,0:T(8,128)}) fusion(f32[512,768]{1,0:T(8,128)} %fusion.6, f32[512,768]{1,0:T(8,128)} %fusion.2, bf16[512,2048]{1,0:T(8,128)(2,1)} %bitcast.4, bf16[1,1,768,2048]{3,2,1,0:T(8,128)(2,1)} %all-gather.7.cloned.1.call-done), kind=kOutput, calls=%fused_computation.18 | convolution fusion | flops 1613364736 | bytes 9962496 | tf_op jit(solution)/shard_map/dot_general | solution.py:20
  135.8 0.7 convert_element_type.113
  136.5 5.9 %all-to-all-start.4 = ((bf16[32,1,16]{2,1,0:T(2,128)(2,1)}), bf16[32,1,16]{2,1,0:T(2,128)(2,1)S(1)}, u32[]{:S(2)}, u32[]{:S(2)}) async-start(bf16[32,1,16]{2,1,0:T(2,128)(2,1)} %convert_element_type.113), calls=%async_computation.4 | async-start | bytes 32768 | tf_op jit(solution)/shard_map/all_to_all | solution.py:125
  142.4 0.0 reduce-scatter.10.cloned.1.call-start
  142.5 0.1 copy.32
  142.6 0.1 broadcast_in_dim.39
  142.7 9.3 %all-to-all-done.4 = bf16[32,1,16]{2,1,0:T(2,128)(2,1)S(1)} async-done(((bf16[32,1,16]{2,1,0:T(2,128)(2,1)}), bf16[32,1,16]{2,1,0:T(2,128)(2,1)S(1)}, u32[]{:S(2)}, u32[]{:S(2)}) %all-to-all-start.4) | async-done | bytes 1056 | tf_op jit(solution)/shard_map/all_to_all | solution.py:125
  152.0 0.1 convert_reduce_fusion
  152.1 0.1 reshape.117
  152.2 0.3 select_reduce_fusion
  152.4 0.1 convert_element_type.112
  152.5 12.7 %all_to_all.27 = bf16[32,1,16]{2,1,0:T(2,128)(2,1)S(1)} all-to-all(bf16[32,1,16]{2,1,0:T(2,128)(2,1)S(1)} %convert_element_type.112), channel_id=1, replica_groups=mesh['section'=4,'dp'=2,'expert'=32] {'expert'}, dimensions={0} | all-to-all | bytes 2048 | tf_op jit(solution)/shard_map/all_to_all | solution.py:84
  165.2 0.1 convert_reduce_fusion.1
  165.3 0.1 reshape.116
  165.4 3.1 %multiply_convert_fusion.1 = (bf16[512,768]{1,0:T(8,128)(2,1)S(1)}, bf16[512,768]{1,0:T(8,128)(2,1)S(1)}) fusion(f32[512,768]{1,0:T(8,128)} %fusion.2, f32[512,768]{1,0:T(8,128)} %get-tuple-element.25, f32[512]{0:T(512)S(1)} %reshape.116, f32[512,768]{1,0:T(8,128)} %fusion.6), kind=kLoop, calls=%fused_computation.20 | loop fusion | flops 5505024 | bytes 6293504 | tf_op jit(solution)/shard_map/convert_element_type | solution.py:28
  168.5 0.9 copy-done.2
  169.4 3.5 %convolution_convert_fusion.2 = bf16[2048,768]{1,0:T(8,128)(2,1)} fusion(bf16[512,2048]{1,0:T(8,128)(2,1)S(1)} %bitcast.77, bf16[512,768]{1,0:T(8,128)(2,1)S(1)} %get-tuple-element.23), kind=kOutput, calls=%fused_computation.3 | convolution fusion | flops 1612185600 | bytes 6029312 | tf_op jit(solution)/shard_map/dot_general | solution.py:32
  172.8 4.8 %copy.36 = bf16[2048,768]{0,1:T(8,128)(2,1)} copy(bf16[2048,768]{1,0:T(8,128)(2,1)} %convolution_convert_fusion.2) | data formatting | bytes 6291456
  177.6 0.0 reduce-scatter.10.cloned.1.call-update
  177.6 0.0 reduce-scatter.12.cloned.1.call-start
  177.7 3.5 %convolution_convert_fusion.1 = bf16[2048,768]{1,0:T(8,128)(2,1)} fusion(bf16[512,2048]{1,0:T(8,128)(2,1)S(1)} %bitcast.78, bf16[512,768]{1,0:T(8,128)(2,1)S(1)} %get-tuple-element.22), kind=kOutput, calls=%fused_computation.2 | convolution fusion | flops 1612185600 | bytes 6029312 | tf_op jit(solution)/shard_map/dot_general | solution.py:35
  181.2 4.9 %copy.38 = bf16[2048,768]{0,1:T(8,128)(2,1)} copy(bf16[2048,768]{1,0:T(8,128)(2,1)} %convolution_convert_fusion.1) | data formatting | bytes 6291456
  186.1 0.0 reduce-scatter.12.cloned.1.call-update
  186.1 0.0 reduce-scatter.8.cloned.1.call-start
  186.2 1.4 copy-done.1
  187.6 5.8 %convolution_convert_fusion = bf16[768,2048]{1,0:T(8,128)(2,1)} fusion(bf16[512,2048]{1,0:T(8,128)(2,1)} %bitcast.4, f32[512]{0:T(512)S(1)} %reshape.116, f32[512,768]{1,0:T(8,128)} %fusion.6, f32[512,768]{1,0:T(8,128)S(1)} %copy-done.1), kind=kOutput, calls=%fused_computation.1 | convolution fusion | flops 1614938112 | bytes 8390656 | tf_op jit(solution)/shard_map/dot_general | solution.py:36
  193.4 0.0 reduce-scatter.8.cloned.1.call-update
  193.4 1.1 copy-done.3
  194.6 3.9 %fusion = f32[512,2048]{1,0:T(8,128)S(1)} fusion(bf16[512,768]{1,0:T(8,128)(2,1)S(1)} %copy-done.3, bf16[1,1,2048,768]{3,2,1,0:T(8,128)(2,1)} %all-gather.11.cloned.1.call-done), kind=kOutput, calls=%fused_computation.4 | convolution fusion | flops 1610612736 | bytes 8126464 | tf_op jit(solution)/shard_map/dot_general | solution.py:29
  198.4 1.9 add_convert_fusion
  200.3 50.5 %all_to_all.28 = bf16[32,16,2048]{2,1,0:T(8,128)(2,1)S(1)} all-to-all(bf16[32,16,2048]{2,1,0:T(8,128)(2,1)S(1)} %bitcast.79), channel_id=1, replica_groups=mesh['section'=4,'dp'=2,'expert'=32] {'expert'}, dimensions={0} | all-to-all | bytes 4194304 | tf_op jit(solution)/shard_map/all_to_all | solution.py:118
  250.8 0.5 convolution_convert_fusion.5
  251.2 0.4 collective-permute-start
  251.7 0.1 broadcast_in_dim_reshape.2
  251.8 0.6 copy.35
  252.4 8.1 %collective-permute-done = bf16[128,2048]{1,0:T(8,128)(2,1)S(1)} collective-permute-done((bf16[128,2048]{1,0:T(8,128)(2,1)S(1)}, bf16[128,2048]{1,0:T(8,128)(2,1)S(1)}, u32[]{:S(2)}, u32[]{:S(2)}) %collective-permute-start) | collective-permute-done | bytes 524320 | tf_op jit(solution)/shard_map/ppermute | solution.py:9
  260.5 2.6 copy.37
  263.1 2.6 copy.39
  265.7 0.8 copy.43
  (20 shorter events, 0.1 us)
Async XLA Ops:
  7.2 3.1 %copy-start = (bf16[1,128,2048]{2,1,0:T(8,128)(2,1)S(1)}, bf16[1,128,2048]{2,1,0:T(8,128)(2,1)}, u32[]{:S(2)}) copy-start(bf16[1,128,2048]{2,1,0:T(8,128)(2,1)} %param.7) | copy-start | bytes 1572868
  7.2 73.7 %all-gather.11.cloned.1.call-start = ((), (), s32[]{:S(2)}) async-start(), calls=%async_computation.11 | async-start | bytes 4718592 | tf_op jit(solution)/shard_map/all_gather | solution.py:99
  12.3 12.4 %copy-start.4 = (bf16[1,128,2048]{2,1,0:T(8,128)(2,1)S(1)}, bf16[1,128,2048]{2,1,0:T(8,128)(2,1)}, u32[]{:S(2)}) copy-start(bf16[1,128,2048]{2,1,0:T(8,128)(2,1)} %param.8) | copy-start | bytes 1572868
  12.3 61.8 %all-to-all-start.2 = ((bf16[32,16,2048]{2,1,0:T(8,128)(2,1)}), bf16[32,16,2048]{2,1,0:T(8,128)(2,1)S(1)}, u32[]{:S(2)}, u32[]{:S(2)}) async-start(bf16[32,16,2048]{2,1,0:T(8,128)(2,1)} %bitcast.7), calls=%async_computation.2 | async-start | bytes 4194304 | tf_op jit(solution)/shard_map/all_to_all | solution.py:70
  23.9 61.8 %all-gather.9.cloned.1.call-start = ((), (), s32[]{:S(2)}) async-start(), calls=%async_computation.10 | async-start | bytes 4718592 | tf_op jit(solution)/shard_map/all_gather | solution.py:100
  74.1 55.2 %all-to-all-start.1 = ((bf16[32,16,2048]{2,1,0:T(8,128)(2,1)}), bf16[32,16,2048]{2,1,0:T(8,128)(2,1)}, u32[]{:S(2)}, u32[]{:S(2)}) async-start(bf16[32,16,2048]{2,1,0:T(8,128)(2,1)} %bitcast.3), calls=%async_computation.1 | async-start | bytes 4194304 | tf_op jit(solution)/shard_map/all_to_all | solution.py:77
  80.2 21.3 %all-gather.7.cloned.1.call-start = ((), (), s32[]{:S(2)}) async-start(), calls=%async_computation.9 | async-start | bytes 4718592 | tf_op jit(solution)/shard_map/all_gather | solution.py:101
  129.3 13.2 %copy-start.5 = (f32[1,128,2]{1,2,0:T(2,128)S(1)}, f32[1,128,2]{1,2,0:T(2,128)}, u32[]{:S(2)}) copy-start(f32[1,128,2]{1,2,0:T(2,128)} %param.10) | copy-start | bytes 3076
  136.5 15.6 %all-to-all-start.4 = ((bf16[32,1,16]{2,1,0:T(2,128)(2,1)}), bf16[32,1,16]{2,1,0:T(2,128)(2,1)S(1)}, u32[]{:S(2)}, u32[]{:S(2)}) async-start(bf16[32,1,16]{2,1,0:T(2,128)(2,1)} %convert_element_type.113), calls=%async_computation.4 | async-start | bytes 32768 | tf_op jit(solution)/shard_map/all_to_all | solution.py:125
  142.4 118.1 %reduce-scatter.10.cloned.1.call-start = ((), (), s32[]{:S(2)}) async-start(), calls=%async_computation.12 | async-start | bytes 4718592
  168.5 0.9 copy-start.2
  177.6 85.5 %reduce-scatter.12.cloned.1.call-start = ((), (), s32[]{:S(2)}) async-start(), calls=%async_computation.13 | async-start | bytes 4718592
  186.1 1.5 copy-start.1
  186.1 79.5 %reduce-scatter.8.cloned.1.call-start = ((), (), s32[]{:S(2)}) async-start(), calls=%async_computation.8 | async-start | bytes 4718592 | tf_op jit(solution)/shard_map/reduce_scatter | solution.py:113
  193.4 1.1 copy-start.3
  194.6 3.9 %copy-start.6 = (bf16[1,1,2048,768]{3,2,1,0:T(8,128)(2,1)S(1)}, bf16[1,1,2048,768]{3,2,1,0:T(8,128)(2,1)}, u32[]{:S(2)}) copy-start(bf16[1,1,2048,768]{3,2,1,0:T(8,128)(2,1)} %all-gather.9.cloned.1.call-done) | copy-start | bytes 9437188
  251.2 9.3 %collective-permute-start = (bf16[128,2048]{1,0:T(8,128)(2,1)S(1)}, bf16[128,2048]{1,0:T(8,128)(2,1)S(1)}, u32[]{:S(2)}, u32[]{:S(2)}) collective-permute-start(bf16[128,2048]{1,0:T(8,128)(2,1)S(1)} %convolution_convert_fusion.5), channel_id=1, source_target_pairs={{0,192},{64,0},{128,64},{192,128},{1,193},{65,1},{129,65},{193,129... | collective-permute-start | bytes 1572872 | tf_op jit(solution)/shard_map/ppermute | solution.py:9
Sparse Core Ops, SparseCore 0:
  9.8 20.3 all-gather.10
  32.0 18.6 all-gather.8
  82.8 18.6 all-gather.6
  177.7 10.6 reduce-scatter.9
  190.9 17.5 reduce-scatter.11
  211.4 17.5 reduce-scatter.7
where the time goes:
time: 275 us; the launch traced here: 273 us
  waiting for transfers between devices  106 us (39%)
  blocking collectives  63.2 us (23%)
  matrix products  39.1 us (14%)
  starting transfers between devices  24.3 us (9%)
  local copies, waits for them, and re-layouts  22.5 us (8%)
  between operations  14.3 us (5%)
  other arithmetic  4.3 us (2%)
    all_to_all x1, blocking collectives, per_device(): lax.all_to_all(route_dx.astype(jnp.bfloat16).reshape(groups, capacity, ro...  50.5 us
    all_to_all x1, waiting for transfers between devices, per_device(): lax.all_to_all(send_rows.reshape(groups, capacity, row_width), 'expert',...  47.4 us
    all_to_all x1, waiting for transfers between devices, per_device(): lax.all_to_all(send_grads.reshape(groups, capacity, row_width), 'expert',...  27.8 us
    unnamed x22, local copies, waits for them, and re-layouts  20.6 us
    all_to_all x1, blocking collectives, per_device(): lax.all_to_all(send_probs.reshape(groups, capacity).astype(jnp.bfloat16),...  12.7 us
    all_to_all x1, starting transfers between devices, per_device(): lax.all_to_all(send_rows.reshape(groups, capacity, row_width), 'expert',...  11.6 us
    all_gather x1, waiting for transfers between devices, per_device(): lax.all_gather(down_part, 'dp', axis=0, tiled=True)  10.9 us
    all_to_all x1, waiting for transfers between devices, per_device(): lax.all_to_all(prob_part.reshape(groups, capacity).astype(jnp.bfloat16),...  9.33 us
  transfers between devices with their start and end apart: 10, of which 5 were waited for; matrix products, arithmetic and copies ran while one was open for 16% of the time, Pallas kernels for 0%

commit v1 on v0

v1 whole, which is shorter than its diff:
```python
import functools

import jax
import jax.numpy as jnp
from jax import lax
from jax.experimental import pallas as pl
from jax.experimental.pallas import tpu as pltpu
from jax.sharding import PartitionSpec as P

MESH = pl.DeviceIdType.MESH
NY = 4
NZ = 8
CAP = 16
ROWS = 128
SLOTS = NY * CAP
F32 = jnp.float32
BF16 = jnp.bfloat16
NT = (((1,), (1,)), ((), ()))
TN = (((0,), (0,)), ((), ()))


def block(direction, distance):
    if distance == 0:
        return 0
    if distance == 4:
        return 7
    return 2 * distance - 1 + direction


def row_base(b):
    if b == 0:
        return 0
    if b == 7:
        return SLOTS
    return ((b + 1) // 2) * 2 * SLOTS + ((b + 1) % 2) * SLOTS


def kernel(
    meta_ref, t_ref, g_ref, wg_hbm, wu_hbm, wd_hbm,
    gi_out, pg_out, og_out, ou_out, od_out,
    gt, gg, gm, tp, gp, pp, rt, rg, rp, wg, wu, wd,
    a_gate, a_up, a_act, dx, pr, yx, yp, sx, rx, sp, rpp, fin,
    wsg, wsu, wsd, wrg, wru, wrd, wog, wou, wod,
    ring_s, ring_r, meta_s, meta_r, disp_s, disp_r, back_s, back_r,
    red_s, red_r, redp_s, redp_r, fin_s, fin_r, w_l, w_s, w_r, wx_s, wx_r, wo_s,
):
    d_model = t_ref.shape[1]
    hid = wg_hbm.shape[1]
    full = 2 * hid
    me = lax.axis_index("expert")
    core = lax.axis_index("dp")
    sec = lax.axis_index("section")
    n_sec = lax.axis_size("section")
    y = lax.rem(me, NY)
    z = me // NY
    ring_to = ({"expert": lax.rem(z + 1, NZ) * NY + y}, {"expert": lax.rem(z + NZ - 1, NZ) * NY + y})
    y_to = [{"expert": z * NY + lax.rem(y + i, NY)} for i in range(NY)]
    twin = {"dp": 1 - core}
    x_prev = {"section": lax.rem(sec + n_sec - 1, n_sec)}
    x_next = {"section": lax.rem(sec + 1, n_sec)}
    pending = []

    def remote(src, dst, ssem, rsem, dev):
        return pltpu.make_async_remote_copy(
            src_ref=src, dst_ref=dst, send_sem=ssem, recv_sem=rsem, device_id=dev, device_id_type=MESH)

    def send(copy):
        copy.start()
        pending.append(copy)

    barrier = pltpu.get_barrier_semaphore()
    greet = [ring_to[0], ring_to[1], y_to[1], y_to[2], y_to[3], twin, x_prev, x_next]
    for dev in greet:
        pl.semaphore_signal(barrier, inc=1, device_id=dev, device_id_type=MESH)

    local_w = [
        pltpu.make_async_copy(wg_hbm, wg.at[:, pl.ds(0, hid)], w_l.at[0]),
        pltpu.make_async_copy(wu_hbm, wu.at[:, pl.ds(0, hid)], w_l.at[1]),
        pltpu.make_async_copy(wd_hbm, wd.at[pl.ds(0, hid)], w_l.at[2]),
    ]
    for copy in local_w:
        copy.start()

    ids = meta_ref[0:2, :]
    experts = lax.broadcasted_iota(jnp.int32, (NY * NZ, ROWS), 0).astype(F32)
    hit0 = jnp.where(experts == ids[0:1, :], 1.0, 0.0)
    hit1 = jnp.where(experts == ids[1:2, :], 1.0, 0.0)
    earlier = jnp.where(
        lax.broadcasted_iota(jnp.int32, (ROWS, ROWS), 0) < lax.broadcasted_iota(jnp.int32, (ROWS, ROWS), 1), 1.0, 0.0
    ).astype(BF16)
    before = jnp.dot((hit0 + hit1).astype(BF16), earlier, preferred_element_type=F32)
    slot0 = ids[0:1, :] * CAP + jnp.sum(hit0 * before, axis=0, keepdims=True)
    slot1 = ids[1:2, :] * CAP + jnp.sum(hit1 * before, axis=0, keepdims=True)
    gm[0] = jnp.concatenate([slot0, slot1, meta_ref[2:8, :]], axis=0)

    pl.semaphore_wait(barrier, len(greet))

    def meta_copy(d, k):
        src = gm.at[0] if k == 1 else gm.at[block(d, k - 1)]
        return remote(src, gm.at[block(d, k)], meta_s.at[d, k - 1], meta_r.at[d, k - 1], ring_to[d])

    def ring_copy(x, d, k):
        own, held = ((t_ref, gt), (g_ref, gg))[x]
        rows = pl.ds(d * (ROWS // 2), ROWS // 2) if k == 4 else pl.ds(0, ROWS)
        src = own.at[rows] if k == 1 else held.at[block(d, k - 1) - 1, rows]
        return remote(src, held.at[block(d, k) - 1, rows], ring_s.at[x, d, k - 1], ring_r.at[x, d, k - 1], ring_to[d])

    for d in range(2):
        send(meta_copy(d, 1))
    for x in range(2):
        for d in range(2):
            send(ring_copy(x, d, 1))
    w_copies = [
        remote(wg_hbm, wg.at[:, pl.ds(hid, hid)], w_s.at[0], w_r.at[0], twin),
        remote(wu_hbm, wu.at[:, pl.ds(hid, hid)], w_s.at[1], w_r.at[1], twin),
        remote(wd_hbm, wd.at[pl.ds(hid, hid)], w_s.at[2], w_r.at[2], twin),
    ]
    for copy in w_copies:
        send(copy)

    slot_row = lax.broadcasted_iota(jnp.int32, (SLOTS, ROWS), 0)
    target = ((z * NY + lax.rem(y + slot_row // CAP, NY)) * CAP + lax.rem(slot_row, CAP)).astype(F32)

    def one_hot(b):
        meta = gm[b]
        return meta[0:1, :] == target, meta[1:2, :] == target

    def disp_copy(b, i, x):
        staged, landed = ((tp, rt), (gp, rg), (pp, rp))[x]
        src = staged.at[b, pl.ds(i * CAP, CAP)]
        dst = landed.at[pl.ds(row_base(b) + (NY - i) * CAP, CAP)]
        return remote(src, dst, disp_s.at[b, i - 1, x], disp_r.at[b, i - 1, x], y_to[i])

    def pack(b, x):
        oh0, oh1 = one_hot(b)
        if x == 2:
            probs = gm[b]
            chosen = jnp.where(oh0, probs[2:3, :], 0.0) + jnp.where(oh1, probs[3:4, :], 0.0)
            spread = jnp.broadcast_to(jnp.sum(chosen, axis=1, keepdims=True), (SLOTS, ROWS))
            pp[b] = spread
            rp[row_base(b):row_base(b) + CAP, :] = spread[0:CAP, :]
        else:
            own, held, staged, landed = ((t_ref, gt, tp, rt), (g_ref, gg, gp, rg))[x]
            hot = (jnp.where(oh0, 1.0, 0.0) + jnp.where(oh1, 1.0, 0.0)).astype(BF16)
            rows = own[...] if b == 0 else held[b - 1]
            packed = jnp.dot(hot, rows, preferred_element_type=F32).astype(BF16)
            staged[b] = packed
            landed[row_base(b):row_base(b) + CAP, :] = packed[0:CAP, :]
        for i in range(1, NY):
            send(disp_copy(b, i, x))

    def landed(b):
        for i in range(1, NY):
            for x in range(3):
                disp_copy(b, i, x).wait_recv()

    def back_copy(b, i, x):
        src, dst = ((dx, yx), (pr, yp))[x]
        return remote(
            src.at[pl.ds(row_base(b) + (NY - i) * CAP, CAP)], dst.at[b, pl.ds(i * CAP, CAP)],
            back_s.at[b, i - 1, x], back_r.at[b, i - 1, x], y_to[NY - i])

    def chunk(c, blocks):
        rows = pl.ds(c * 2 * SLOTS, 2 * SLOTS)
        for b in blocks:
            landed(b)
        pr[rows, :] = jnp.zeros((2 * SLOTS, ROWS), F32)
        tile = 256

        @pl.loop(0, full // tile)
        def _(n):
            cols = pl.ds(pl.multiple_of(n * tile, tile), tile)
            tok = rt[rows, :]
            grd = rg[rows, :]
            gate = jnp.dot(tok, wg[:, cols], preferred_element_type=F32)
            up = jnp.dot(tok, wu[:, cols], preferred_element_type=F32)
            hidden = lax.dot_general(grd, wd[cols, :], NT, preferred_element_type=F32)
            prob = rp[rows, :][:, 0:1]
            sig = jax.nn.sigmoid(gate)
            silu = gate * sig
            act = silu * up
            a_act[rows, cols] = (prob * act).astype(BF16)
            pr[rows, :] += jnp.broadcast_to(jnp.sum(act * hidden, axis=1, keepdims=True), (2 * SLOTS, ROWS))
            scaled = prob * hidden
            a_gate[rows, cols] = (scaled * up * sig * (1.0 + gate * (1.0 - sig))).astype(BF16)
            a_up[rows, cols] = (scaled * silu).astype(BF16)

        tile_d = 512

        @pl.loop(0, d_model // tile_d)
        def _(n):
            cols = pl.ds(pl.multiple_of(n * tile_d, tile_d), tile_d)
            out = lax.dot_general(a_gate[rows, :], wg[cols, :], NT, preferred_element_type=F32)
            out += lax.dot_general(a_up[rows, :], wu[cols, :], NT, preferred_element_type=F32)
            dx[rows, cols] = out.astype(BF16)

        for b in blocks:
            for i in range(1, NY):
                for x in range(2):
                    send(back_copy(b, i, x))
            yx[b, 0:CAP, :] = dx[row_base(b):row_base(b) + CAP, :]
            yp[b, 0:CAP, :] = pr[row_base(b):row_base(b) + CAP, :]

    for x in (2, 0, 1):
        pack(0, x)
    for k in range(1, 4):
        for d in range(2):
            meta_copy(d, k).wait_recv()
            if k < 3 or d == 0:
                send(meta_copy(d, k + 1))
        for x in range(2):
            for d in range(2):
                ring_copy(x, d, k).wait_recv()
                send(ring_copy(x, d, k + 1))
        for d in range(2):
            for x in (2, 0, 1):
                pack(block(d, k), x)
        if k == 1:
            for copy in local_w:
                copy.wait()
            for copy in w_copies:
                copy.wait_recv()
        else:
            chunk(k - 1, (block(0, k - 1), block(1, k - 1)))
    meta_copy(0, 4).wait_recv()
    for d in range(2):
        ring_copy(0, d, 4).wait_recv()
    pack(7, 2)
    pack(7, 0)
    chunk(3, (block(0, 3), block(1, 3)))
    for d in range(2):
        ring_copy(1, d, 4).wait_recv()
    pack(7, 1)
    chunk(0, (0, 7))

    half_cols = d_model // 2
    half_rows = ROWS // 2

    def red_copy(d, m, s):
        rows = pl.ds(d * half_rows, half_rows) if m == 1 else pl.ds(0, ROWS)
        cols = pl.ds(s * half_cols, half_cols)
        return remote(
            sx.at[d, m - 1, rows, cols], rx.at[d, m - 1, rows, cols],
            red_s.at[d, m - 1, s], red_r.at[d, m - 1, s], ring_to[d])

    def redp_copy(d, m):
        return remote(sp.at[d, m - 1], rpp.at[d, m - 1], redp_s.at[d, m - 1], redp_r.at[d, m - 1], ring_to[d])

    def back_landed(b):
        for i in range(1, NY):
            for x in range(2):
                back_copy(b, i, x).wait_recv()

    def prob_part(b):
        oh0, oh1 = one_hot(b)
        val = yp[b]
        p0 = jnp.sum(jnp.where(oh0, val, 0.0), axis=0, keepdims=True)
        p1 = jnp.sum(jnp.where(oh1, val, 0.0), axis=0, keepdims=True)
        return jnp.concatenate([p0, p1, jnp.zeros((6, ROWS), F32)], axis=0)

    def spread_rows(b, s):
        oh0, oh1 = one_hot(b)
        hot = (jnp.where(oh0, 1.0, 0.0) + jnp.where(oh1, 1.0, 0.0)).astype(BF16)
        return lax.dot_general(hot, yx[b, :, s * half_cols:(s + 1) * half_cols], TN, preferred_element_type=F32)

    def stage(m):
        for d in range(2):
            b = block(1 - d, 5 - m)
            if m > 1 or d == 0:
                back_landed(b)
        for s in range(2):
            cols = slice(s * half_cols, (s + 1) * half_cols)
            for d in range(2):
                b = block(1 - d, 5 - m)
                part = spread_rows(b, s)
                if m == 1:
                    rows = slice(d * half_rows, (d + 1) * half_rows)
                    sx[d, 0, rows, cols] = part[rows].astype(BF16)
                else:
                    red_copy(d, m - 1, s).wait_recv()
                    if m == 2:
                        rows = slice(d * half_rows, (d + 1) * half_rows)
                        rest = slice((1 - d) * half_rows, (2 - d) * half_rows)
                        sx[d, 1, rows, cols] = (part[rows] + rx[d, 0, rows, cols].astype(F32)).astype(BF16)
                        sx[d, 1, rest, cols] = part[rest].astype(BF16)
                    else:
                        sx[d, m - 1, :, cols] = (part + rx[d, m - 2, :, cols].astype(F32)).astype(BF16)
                send(red_copy(d, m, s))
        for d in range(2):
            if m == 1 and d == 1:
                continue
            val = prob_part(block(1 - d, 5 - m))
            if m > 2 or (m == 2 and d == 0):
                redp_copy(d, m - 1).wait_recv()
                val = val + rpp[d, m - 2]
            sp[d, m - 1] = val
            send(redp_copy(d, m))

    tile = 256

    def grad_gate_up():
        @pl.loop(0, d_model // tile)
        def _(n):
            at = pl.ds(pl.multiple_of(n * tile, tile), tile)
            tok = rt[:, at]
            for acts, other, mine in ((a_gate, wsg, wog), (a_up, wsu, wou)):
                out = lax.dot_general(tok, acts[...], TN, preferred_element_type=F32).astype(BF16)
                mine[at, :] = out[:, 0:hid]
                other[at, :] = out[:, hid:full]

    def grad_down():
        @pl.loop(0, d_model // tile)
        def _(n):
            at = pl.ds(pl.multiple_of(n * tile, tile), tile)
            out = lax.dot_general(a_act[...], rg[:, at], TN, preferred_element_type=F32).astype(BF16)
            wod[:, at] = out[0:hid, :]
            wsd[:, at] = out[hid:full, :]

    trio = ((wsg, wrg, wog, og_out), (wsu, wru, wou, ou_out), (wsd, wrd, wod, od_out))

    def wx_copy(j):
        return remote(trio[j][0], trio[j][1], wx_s.at[j], wx_r.at[j], twin)

    def finish_weight(j):
        wx_copy(j).wait_recv()
        _, got, mine, out = trio[j]
        step = mine.shape[0] // 4

        @pl.loop(0, 4)
        def _(n):
            at = pl.ds(pl.multiple_of(n * step, step), step)
            mine[at, :] = (mine[at, :].astype(F32) + got[at, :].astype(F32)).astype(BF16)

        copy = pltpu.make_async_copy(mine, out, wo_s.at[j])
        copy.start()
        return copy

    stage(1)
    grad_gate_up()
    send(wx_copy(0))
    send(wx_copy(1))
    stage(2)
    grad_down()
    send(wx_copy(2))
    stage(3)
    outs = [finish_weight(0), finish_weight(1)]
    stage(4)
    outs.append(finish_weight(2))

    def fin_copy(s):
        cols = pl.ds(s * half_cols, half_cols)
        return remote(fin.at[:, cols], gi_out.at[:, cols], fin_s.at[s], fin_r.at[s], x_prev)

    back_landed(0)
    for s in range(2):
        cols = slice(s * half_cols, (s + 1) * half_cols)
        part = spread_rows(0, s)
        for d in range(2):
            red_copy(d, 4, s).wait_recv()
        part = part + rx[0, 3, :, cols].astype(F32) + rx[1, 3, :, cols].astype(F32)
        fin[:, cols] = part.astype(BF16)
        send(fin_copy(s))
    for d in range(2):
        redp_copy(d, 4).wait_recv()
    pg_out[...] = prob_part(0) + rpp[0, 3] + rpp[1, 3]
    for s in range(2):
        fin_copy(s).wait_recv()
    for copy in pending:
        copy.wait_send()
    for copy in outs:
        copy.wait()


def per_device(tokens, out_grad, expert_ids, route_probs, gate_weight, up_weight, down_weight):
    rows, d_model = tokens.shape[1:]
    hid = gate_weight.shape[3]
    full = 2 * hid
    meta = jnp.concatenate(
        [expert_ids[0].astype(F32).T, route_probs[0].T, jnp.zeros((4, rows), F32)], axis=0)
    vmem = pltpu.VMEM
    dma = pltpu.SemaphoreType.DMA
    in_vmem = pl.BlockSpec(memory_space=pltpu.VMEM)
    anywhere = pl.BlockSpec(memory_space=pl.ANY)
    n_slots = NZ * SLOTS
    scratch = [
        vmem((7, ROWS, d_model), BF16), vmem((7, ROWS, d_model), BF16), vmem((8, 8, ROWS), F32),
        vmem((8, SLOTS, d_model), BF16), vmem((8, SLOTS, d_model), BF16), vmem((8, SLOTS, ROWS), F32),
        vmem((n_slots, d_model), BF16), vmem((n_slots, d_model), BF16), vmem((n_slots, ROWS), F32),
        vmem((d_model, full), BF16), vmem((d_model, full), BF16), vmem((full, d_model), BF16),
        vmem((n_slots, full), BF16), vmem((n_slots, full), BF16), vmem((n_slots, full), BF16),
        vmem((n_slots, d_model), BF16), vmem((n_slots, ROWS), F32),
        vmem((8, SLOTS, d_model), BF16), vmem((8, SLOTS, ROWS), F32),
        vmem((2, 4, ROWS, d_model), BF16), vmem((2, 4, ROWS, d_model), BF16),
        vmem((2, 4, 8, ROWS), F32), vmem((2, 4, 8, ROWS), F32),
        vmem((ROWS, d_model), BF16),
        vmem((d_model, hid), BF16), vmem((d_model, hid), BF16), vmem((hid, d_model), BF16),
        vmem((d_model, hid), BF16), vmem((d_model, hid), BF16), vmem((hid, d_model), BF16),
        vmem((d_model, hid), BF16), vmem((d_model, hid), BF16), vmem((hid, d_model), BF16),
        dma((2, 2, 4)), dma((2, 2, 4)), dma((2, 4)), dma((2, 4)),
        dma((8, 3, 3)), dma((8, 3, 3)), dma((8, 3, 2)), dma((8, 3, 2)),
        dma((2, 4, 2)), dma((2, 4, 2)), dma((2, 4)), dma((2, 4)),
        dma((2,)), dma((2,)), dma((3,)), dma((3,)), dma((3,)), dma((3,)), dma((3,)), dma((3,)),
    ]
    grad_in, prob, grad_gate, grad_up, grad_down = pl.pallas_call(
        kernel,
        out_shape=(
            jax.ShapeDtypeStruct((rows, d_model), BF16), jax.ShapeDtypeStruct((8, rows), F32),
            jax.ShapeDtypeStruct((d_model, hid), BF16), jax.ShapeDtypeStruct((d_model, hid), BF16),
            jax.ShapeDtypeStruct((hid, d_model), BF16)),
        in_specs=[in_vmem, in_vmem, in_vmem, anywhere, anywhere, anywhere],
        out_specs=(anywhere, in_vmem, anywhere, anywhere, anywhere),
        scratch_shapes=scratch,
        compiler_params=pltpu.CompilerParams(
            collective_id=0, has_side_effects=True, vmem_limit_bytes=62 * 1024 * 1024),
    )(meta, tokens[0], out_grad[0], gate_weight[0, 0], up_weight[0, 0], down_weight[0, 0])
    return (
        grad_in[None], prob[0:2].T[None], grad_gate[None, None], grad_up[None, None], grad_down[None, None])


def solution(mesh):
    in_specs = (
        P("section", ("dp", "expert"), None), P("section", ("dp", "expert"), None),
        P("section", ("dp", "expert"), None), P("section", ("dp", "expert"), None),
        P("section", "expert", None, "dp"), P("section", "expert", None, "dp"), P("section", "expert", "dp", None))
    out_specs = (
        P("section", ("dp", "expert"), None), P("section", ("dp", "expert"), None),
        P("section", "expert", None, "dp"), P("section", "expert", None, "dp"), P("section", "expert", "dp", None))
    return jax.shard_map(per_device, mesh=mesh, in_specs=in_specs, out_specs=out_specs, check_vma=False)
```

time: 275 us -> 186 us (0.68)
  Pallas kernels: 0 us -> 174 us
  waiting for transfers between devices: 106 us -> 0 us
  blocking collectives: 63.2 us -> 0 us
  matrix products: 39.1 us -> 0 us
  starting transfers between devices: 24.3 us -> 0 us
  between operations: 14.3 us -> 0.65 us
  local copies, waits for them, and re-layouts: 22.5 us -> 9.15 us
    pallas_call x0 -> x1, Pallas kernels: none -> 174 us  [per_device(): pl.pallas_call(kernel, out_shape=(jax.ShapeDtypeStruct((rows, d_model), B...]
    all_to_all x3 -> x0, waiting for transfers between devices: 84.6 us -> none  [the longest x1 47.4 us: per_device(): lax.all_to_all(send_rows.reshape(groups, capacity, row_width), 'expert',...]
    all_to_all x2 -> x0, blocking collectives: 63.2 us -> none  [the longest x1 50.5 us: per_device(): lax.all_to_all(route_dx.astype(jnp.bfloat16).reshape(groups, capacity, ro...]
    dot_general x11 -> x0, matrix products: 39.1 us -> none  [the longest x1 6.46 us: expert_grads(): lax.dot_general(grads_in, down_part, contract_last, preferred_element_typ...]
    all_to_all x3 -> x0, starting transfers between devices: 23.6 us -> none  [the longest x1 11.6 us: per_device(): lax.all_to_all(send_rows.reshape(groups, capacity, row_width), 'expert',...]
    unnamed x22 -> x8, local copies, waits for them, and re-layouts: 20.6 us -> 7.83 us
    all_gather x3 -> x0, waiting for transfers between devices: 10.9 us -> none  [the longest x1 10.9 us: per_device(): lax.all_gather(down_part, 'dp', axis=0, tiled=True)]
    ppermute x1 -> x0, waiting for transfers between devices: 8.07 us -> none  [from_behind(): lax.ppermute(shard, axis, [(i, (i + by) % length) for i in range(length)])]
  transfers between devices with their start and end apart: 10 -> 0, of which waited for: 5 -> 0; matrix products, arithmetic and copies ran while one was open for 16% -> 0% of each run, Pallas kernels for 0% -> 0%
where the time goes in v1:
time: 186 us; the launch traced here: 185 us
  Pallas kernels  174 us (94%)
  local copies, waits for them, and re-layouts  9.15 us (5%)
  other arithmetic  2.02 us (1%)
    pallas_call x1, Pallas kernels, per_device(): pl.pallas_call(kernel, out_shape=(jax.ShapeDtypeStruct((rows, d_model), B...  174 us
    unnamed x8, local copies, waits for them, and re-layouts  7.83 us

profile of v1, /device:TPU:2, one launch (start us, length us, event | category | flops | bytes accessed | tf_op | source)
XLA Modules:
  0.0 185.5 jit_solution(10995522015168738622)
XLA Ops:
  0.6 0.1 pad.2.clone
  0.7 0.7 convert_bitcast_fusion
  1.4 1.3 maximum_maximum_fusion.meta_ref
  2.7 173.7 %shard_map.110 = (bf16[128,2048]{1,0:T(8,128)(2,1)}, f32[8,128]{1,0:T(8,128)}, bf16[2048,384]{1,0:T(8,128)(2,1)}, bf16[2048,384]{1,0:T(8,128)(2,1)}, bf16[384,2048]{1,0:T(8,128)(2,1)}) custom-call(f32[8,128]{1,0:T(8,128)} %maximum_maximum_fusion.meta_ref, bf16[128,2048]{1,0:T(8,128)(2,1)} %bitcast.26, bf16[128,2048]{1,0:T(8,128)(2,1)} %bitcast.27, ...), custom_call_target="tpu_custom_call" | custom-call | tf_op jit(solution)/shard_map/pallas_call | solution.py:404
  176.4 1.2 slice_bitcast_fusion
  177.7 1.9 %copy.16 = bf16[1,128,2048]{2,1,0:T(8,128)(2,1)} copy(bf16[1,128,2048]{2,1,0:T(8,128)(2,1)} %bitcast.28) | data formatting | bytes 1048576
  179.5 0.0 copy-start.1
  179.5 2.8 %copy.17 = bf16[1,1,2048,384]{3,2,1,0:T(8,128)(2,1)} copy(bf16[1,1,2048,384]{3,2,1,0:T(8,128)(2,1)} %bitcast.22) | data formatting | bytes 3145728
  182.4 0.0 copy-done.1
  182.4 0.0 copy-start
  182.4 1.1 copy.18
  183.5 0.8 copy-done
  184.4 1.1 copy.19
  (1 shorter events, 0.0 us)
Async XLA Ops:
  179.5 2.8 %copy-start.1 = (bf16[2048,384]{1,0:T(8,128)(2,1)S(1)}, bf16[2048,384]{1,0:T(8,128)(2,1)}, u32[]{:S(2)}) copy-start(bf16[2048,384]{1,0:T(8,128)(2,1)} %get-tuple-element.13) | copy-start | bytes 4718596
  182.4 2.0 %copy-start = (bf16[384,2048]{1,0:T(8,128)(2,1)S(1)}, bf16[384,2048]{1,0:T(8,128)(2,1)}, u32[]{:S(2)}) copy-start(bf16[384,2048]{1,0:T(8,128)(2,1)} %get-tuple-element.14) | copy-start | bytes 4718596

commit v2 on v1

v2 whole, which is shorter than its diff:
```python
import jax
import jax.numpy as jnp
from jax import lax
from jax.experimental import pallas as pl
from jax.experimental.pallas import tpu as pltpu
from jax.sharding import PartitionSpec as P

MESH = pl.DeviceIdType.MESH
NY = 4
NZ = 8
CAP = 16
ROWS = 128
SLOTS = NY * CAP
HALF = SLOTS // 2
FAR = SLOTS + HALF
LAST = 3 * SLOTS
PARTS = 4
F32 = jnp.float32
BF16 = jnp.bfloat16
NT = (((1,), (1,)), ((), ()))
TN = (((0,), (0,)), ((), ()))


def block(direction, distance):
    if distance == 0:
        return 0
    if distance == 4:
        return 7
    return 2 * distance - 1 + direction


AHEAD = (0, block(1, 1))


def kernel(
    ids_ref, probs_ref, t_ref, g_ref, wg_hbm, wu_hbm, wd_hbm,
    gi_out, pg_out, og_out, ou_out, od_out,
    gt, gg, gm, gmx, tp, gp, pp, fs, fr, rt, rg, rp, wg, wu, wd,
    z_gate, z_up, a_gate, a_up, a_act, dx, pr, yx, yp, f1, f2, sx, rx, sp, rpp, fin,
    wsg, wsu, wsd, wrg, wru, wrd, wog, wou, wod,
    ring_s, ring_r, meta_s, meta_r, mx_s, mx_r, disp_s, disp_r, back_s, back_r,
    red_s, red_r, redp_s, redp_r, fin_s, w_l, w_s, w_r, wx_s, wx_r, wo_s,
):
    d_model = t_ref.shape[1]
    hid = wg_hbm.shape[1]
    full = 2 * hid
    me = lax.axis_index("expert")
    core = lax.axis_index("dp")
    sec = lax.axis_index("section")
    n_sec = lax.axis_size("section")
    y = lax.rem(me, NY)
    z = me // NY
    x_prev = lax.rem(sec + n_sec - 1, n_sec)
    x_next = lax.rem(sec + 1, n_sec)
    ring = (lax.rem(z + 1, NZ) * NY + y, lax.rem(z + NZ - 1, NZ) * NY + y)
    column = [z * NY + lax.rem(y + i, NY) for i in range(NY)]
    ring_to = [{"expert": e} for e in ring]
    ring_x = [{"section": x_prev, "expert": e} for e in ring]
    y_to = [{"expert": e} for e in column]
    y_x = [{"section": x_prev, "expert": e} for e in column]
    twin = {"dp": 1 - core}
    pending = []

    def remote(src, dst, ssem, rsem, dev):
        return pltpu.make_async_remote_copy(
            src_ref=src, dst_ref=dst, send_sem=ssem, recv_sem=rsem, device_id=dev, device_id_type=MESH)

    def send(copy):
        copy.start()
        pending.append(copy)

    barrier = pltpu.get_barrier_semaphore()
    greet = ring_to + y_to[1:] + [twin] + y_x + ring_x
    greet += [{"section": x_next, "expert": e} for e in column + list(ring)]
    for dev in greet:
        pl.semaphore_signal(barrier, inc=1, device_id=dev, device_id_type=MESH)

    local_w = [
        pltpu.make_async_copy(wg_hbm, wg.at[:, pl.ds(0, hid)], w_l.at[0]),
        pltpu.make_async_copy(wu_hbm, wu.at[:, pl.ds(0, hid)], w_l.at[1]),
        pltpu.make_async_copy(wd_hbm, wd.at[pl.ds(0, hid)], w_l.at[2]),
    ]
    for copy in local_w:
        copy.start()

    ids = ids_ref[...].astype(F32)
    experts = lax.broadcasted_iota(jnp.int32, (NY * NZ, ROWS), 0).astype(F32)
    hit0 = jnp.where(experts == ids[0:1, :], 1.0, 0.0)
    hit1 = jnp.where(experts == ids[1:2, :], 1.0, 0.0)
    earlier = jnp.where(
        lax.broadcasted_iota(jnp.int32, (ROWS, ROWS), 0) < lax.broadcasted_iota(jnp.int32, (ROWS, ROWS), 1), 1.0, 0.0
    ).astype(BF16)
    before = jnp.dot((hit0 + hit1).astype(BF16), earlier, preferred_element_type=F32)
    slot0 = ids[0:1, :] * CAP + jnp.sum(hit0 * before, axis=0, keepdims=True)
    slot1 = ids[1:2, :] * CAP + jnp.sum(hit1 * before, axis=0, keepdims=True)
    gm[0] = jnp.concatenate([slot0, slot1, probs_ref[...], jnp.zeros((4, ROWS), F32)], axis=0)

    pl.semaphore_wait(barrier, len(greet))

    def meta_copy(d, k):
        src = gm.at[0] if k == 1 else gm.at[block(d, k - 1)]
        return remote(src, gm.at[block(d, k)], meta_s.at[d, k - 1], meta_r.at[d, k - 1], ring_to[d])

    def metax_copy(j):
        return remote(gm.at[AHEAD[j]], gmx.at[j], mx_s.at[j], mx_r.at[j], {"section": x_prev})

    def ring_copy(x, d, k):
        own, held, staged = ((t_ref, gt, tp), (g_ref, gg, gp))[x]
        if k == 1:
            src, dst = own, held.at[block(d, 1) - 1]
        elif k == 2:
            src, dst = held.at[block(d, 1) - 1], held.at[block(d, 2) - 1]
        elif k == 3:
            src, dst = fs.at[x, d], fr.at[x, d]
        else:
            src, dst = fr.at[x, d, pl.ds(SLOTS, HALF)], staged.at[7, pl.ds(d * HALF, HALF)]
        return remote(src, dst, ring_s.at[x, d, k - 1], ring_r.at[x, d, k - 1], ring_to[d])

    for d in range(2):
        send(meta_copy(d, 1))
    for x in range(2):
        for d in range(2):
            send(ring_copy(x, d, 1))
    send(metax_copy(0))
    w_copies = [
        remote(wg_hbm, wg.at[:, pl.ds(hid, hid)], w_s.at[0], w_r.at[0], twin),
        remote(wu_hbm, wu.at[:, pl.ds(hid, hid)], w_s.at[1], w_r.at[1], twin),
        remote(wd_hbm, wd.at[pl.ds(hid, hid)], w_s.at[2], w_r.at[2], twin),
    ]
    for copy in w_copies:
        send(copy)

    def slot_names(plane, rows, first):
        row = lax.broadcasted_iota(jnp.int32, (rows, ROWS), 0)
        return ((plane * NY + lax.rem(y + first + row // CAP, NY)) * CAP + lax.rem(row, CAP)).astype(F32)

    def matches(meta, names):
        return meta[0:1, :] == names, meta[1:2, :] == names

    def as_hot(pair):
        return (jnp.where(pair[0], 1.0, 0.0) + jnp.where(pair[1], 1.0, 0.0)).astype(BF16)

    def near_hot(meta):
        return as_hot(matches(meta, slot_names(z, SLOTS, 0)))

    def far_hot(d):
        step = 1 if d == 0 else NZ - 1
        names = jnp.concatenate([
            slot_names(lax.rem(z + step, NZ), SLOTS, 0), slot_names(lax.rem(z + 2 * step, NZ), HALF, 2 * d)], axis=0)
        return as_hot(matches(gm[block(d, 2)], names))

    def staged_at(b, x):
        if x == 2:
            return pp.at[b]
        if b in (5, 6):
            return fr.at[x, b - 5]
        return (tp, gp)[x].at[b]

    def disp_copy(b, i, x):
        landing = (rt, rg, rp)[x]
        src = staged_at(b, x).at[pl.ds(i * CAP, CAP)]
        dst = landing.at[pl.ds(b * SLOTS + (NY - i) * CAP, CAP)]
        return remote(src, dst, disp_s.at[b, i - 1, x], disp_r.at[b, i - 1, x], y_to[i])

    def pack(b, x):
        top = slice(b * SLOTS, b * SLOTS + CAP)
        if x == 2:
            meta = gm[b]
            oh0, oh1 = matches(meta, slot_names(z, SLOTS, 0))
            chosen = jnp.where(oh0, meta[2:3, :], 0.0) + jnp.where(oh1, meta[3:4, :], 0.0)
            spread = jnp.broadcast_to(jnp.sum(chosen, axis=1, keepdims=True), (SLOTS, ROWS))
            pp[b] = spread
            rp[top, :] = spread[0:CAP, :]
        elif b < 5:
            own, held, staged, landing = ((t_ref, gt, tp, rt), (g_ref, gg, gp, rg))[x]
            rows = own[...] if b == 0 else held[b - 1]
            packed = jnp.dot(near_hot(gm[b]), rows, preferred_element_type=F32).astype(BF16)
            staged[b] = packed
            landing[top, :] = packed[0:CAP, :]
        for i in range(1, NY):
            send(disp_copy(b, i, x))
        if x < 2 and b >= 5:
            (rt, rg)[x][top, :] = staged_at(b, x)[0:CAP, :]

    def landed(b, x):
        for i in range(1, NY):
            disp_copy(b, i, x).wait_recv()

    def back_copy(b, i, x):
        rows = pl.ds(b * SLOTS + (0 if i == 0 else NY - i) * CAP, CAP)
        src, dst = ((dx, yx), (pr, yp))[x]
        dev = y_x[(NY - i) % NY] if x == 0 and b in AHEAD else y_to[(NY - i) % NY]
        return remote(src.at[rows], dst.at[b, pl.ds(i * CAP, CAP)], back_s.at[b, i, x], back_r.at[b, i, x], dev)

    def back_routes(b, x):
        return range(0 if x == 0 and b in AHEAD else 1, NY)

    def gate_up(first, count):
        tile = 256
        rows = pl.ds(first, count)

        @pl.loop(0, full // tile)
        def _(n):
            cols = pl.ds(pl.multiple_of(n * tile, tile), tile)
            tok = rt[rows, :]
            z_gate[0:count, cols] = jnp.dot(tok, wg[:, cols], preferred_element_type=F32)
            z_up[0:count, cols] = jnp.dot(tok, wu[:, cols], preferred_element_type=F32)

    def hidden_dx(first, count):
        tile = 256
        rows = pl.ds(first, count)
        pr[rows, :] = jnp.zeros((count, ROWS), F32)

        @pl.loop(0, full // tile)
        def _(n):
            cols = pl.ds(pl.multiple_of(n * tile, tile), tile)
            hidden = lax.dot_general(rg[rows, :], wd[cols, :], NT, preferred_element_type=F32)
            gate = z_gate[0:count, cols]
            up = z_up[0:count, cols]
            prob = rp[rows, :][:, 0:1]
            sig = jax.nn.sigmoid(gate)
            silu = gate * sig
            act = silu * up
            a_act[rows, cols] = (prob * act).astype(BF16)
            pr[rows, :] += jnp.broadcast_to(jnp.sum(act * hidden, axis=1, keepdims=True), (count, ROWS))
            scaled = prob * hidden
            a_gate[rows, cols] = (scaled * up * sig * (1.0 + gate * (1.0 - sig))).astype(BF16)
            a_up[rows, cols] = (scaled * silu).astype(BF16)

        tile_d = 512

        @pl.loop(0, d_model // tile_d)
        def _(n):
            cols = pl.ds(pl.multiple_of(n * tile_d, tile_d), tile_d)
            out = lax.dot_general(a_gate[rows, :], wg[cols, :], NT, preferred_element_type=F32)
            out += lax.dot_general(a_up[rows, :], wu[cols, :], NT, preferred_element_type=F32)
            dx[rows, cols] = out.astype(BF16)

    def send_back(blocks):
        for b in blocks:
            for x in range(2):
                for i in back_routes(b, x):
                    send(back_copy(b, i, x))
        for b in blocks:
            top = slice(b * SLOTS, b * SLOTS + CAP)
            if b not in AHEAD:
                yx[b, 0:CAP, :] = dx[top, :]
            yp[b, 0:CAP, :] = pr[top, :]

    def chunk(blocks):
        first, count = blocks[0] * SLOTS, len(blocks) * SLOTS
        for b in blocks:
            for x in (0, 1, 2):
                landed(b, x)
        gate_up(first, count)
        hidden_dx(first, count)
        send_back(blocks)

    for x in (2, 0, 1):
        pack(0, x)
    for d in range(2):
        meta_copy(d, 1).wait_recv()
        send(meta_copy(d, 2))
    for x in range(2):
        for d in range(2):
            ring_copy(x, d, 1).wait_recv()
            send(ring_copy(x, d, 2))
    send(metax_copy(1))
    for d in range(2):
        for x in (2, 0, 1):
            pack(block(d, 1), x)
    for copy in local_w:
        copy.wait()
    for copy in w_copies:
        copy.wait_recv()
    for d in range(2):
        meta_copy(d, 2).wait_recv()
        send(meta_copy(d, 3))
    for x in range(2):
        for d in range(2):
            ring_copy(x, d, 2).wait_recv()
            held = (gt, gg)[x]
            fs[x, d] = jnp.dot(far_hot(d), held[block(d, 2) - 1], preferred_element_type=F32).astype(BF16)
            send(ring_copy(x, d, 3))
        for d in range(2):
            if x == 0:
                pack(block(d, 2), 2)
            pack(block(d, 2), x)
        if x == 0:
            chunk((0, 1, 2))
    for d in range(2):
        meta_copy(d, 3).wait_recv()
        if d == 0:
            send(meta_copy(d, 4))
    for x in range(2):
        for d in range(2):
            ring_copy(x, d, 3).wait_recv()
            send(ring_copy(x, d, 4))
        for d in range(2):
            pack(block(d, 3), x)
        if x == 0:
            for d in range(2):
                pack(block(d, 3), 2)
            chunk((3, 4))
    meta_copy(0, 4).wait_recv()
    pack(7, 2)
    for x in range(2):
        for d in range(2):
            ring_copy(x, d, 4).wait_recv()
        pack(7, x)
    for b in (5, 6, 7):
        landed(b, 0)
    gate_up(5 * SLOTS, LAST)
    for b in (5, 6, 7):
        landed(b, 1)
        landed(b, 2)
    hidden_dx(5 * SLOTS, LAST)
    send_back((7, 5, 6))

    width = d_model // PARTS

    def red_copy(d, m, s):
        cols = pl.ds(s * width, width)
        dev = ring_to[d]
        if m == 0:
            src, dst = yx.at[7, pl.ds((1 - d) * HALF, HALF), cols], f1.at[d, :, cols]
        elif m == 1:
            src, dst = yx.at[block(1 - d, 3), :, cols], f2.at[d, pl.ds(0, SLOTS), cols]
        elif m == 2:
            src, dst = f1.at[d, :, cols], f2.at[d, pl.ds(SLOTS, HALF), cols]
        else:
            src, dst = sx.at[d, m - 3, :, cols], rx.at[d, m - 3, :, cols]
            if m == 3 + d:
                dev = ring_x[d]
        return remote(src, dst, red_s.at[d, m, s], red_r.at[d, m, s], dev)

    def redp_copy(d, m):
        return remote(sp.at[d, m - 1], rpp.at[d, m - 1], redp_s.at[d, m - 1], redp_r.at[d, m - 1], ring_to[d])

    def back_landed(b, x):
        for i in back_routes(b, x):
            back_copy(b, i, x).wait_recv()

    def prob_part(b):
        oh0, oh1 = matches(gm[b], slot_names(z, SLOTS, 0))
        val = yp[b]
        p0 = jnp.sum(jnp.where(oh0, val, 0.0), axis=0, keepdims=True)
        p1 = jnp.sum(jnp.where(oh1, val, 0.0), axis=0, keepdims=True)
        return jnp.concatenate([p0, p1, jnp.zeros((6, ROWS), F32)], axis=0)

    def prob_stage(m):
        for d in range(2):
            if m == 1 and d == 1:
                continue
            b = block(1 - d, 5 - m)
            back_landed(b, 1)
            val = prob_part(b)
            if m > 2 or (m == 2 and d == 0):
                redp_copy(d, m - 1).wait_recv()
                val = val + rpp[d, m - 2]
            sp[d, m - 1] = val
            send(redp_copy(d, m))

    def spread_rows(hot, rows):
        return lax.dot_general(hot, rows, TN, preferred_element_type=F32)

    tile = 256

    def grad_gate_up():
        @pl.loop(0, d_model // tile)
        def _(n):
            at = pl.ds(pl.multiple_of(n * tile, tile), tile)
            tok = rt[:, at]
            for acts, other, mine in ((a_gate, wsg, wog), (a_up, wsu, wou)):
                out = lax.dot_general(tok, acts[...], TN, preferred_element_type=F32).astype(BF16)
                mine[at, :] = out[:, 0:hid]
                other[at, :] = out[:, hid:full]

    def grad_down():
        @pl.loop(0, d_model // tile)
        def _(n):
            at = pl.ds(pl.multiple_of(n * tile, tile), tile)
            out = lax.dot_general(a_act[...], rg[:, at], TN, preferred_element_type=F32).astype(BF16)
            wod[:, at] = out[0:hid, :]
            wsd[:, at] = out[hid:full, :]

    trio = ((wsg, wrg, wog, og_out), (wsu, wru, wou, ou_out), (wsd, wrd, wod, od_out))
    outs = []

    def wx_copy(j):
        return remote(trio[j][0], trio[j][1], wx_s.at[j], wx_r.at[j], twin)

    def finish_weight(j):
        wx_copy(j).wait_recv()
        _, got, mine, out = trio[j]
        step = mine.shape[0] // 4

        @pl.loop(0, 4)
        def _(n):
            at = pl.ds(pl.multiple_of(n * step, step), step)
            mine[at, :] = (mine[at, :].astype(F32) + got[at, :].astype(F32)).astype(BF16)

        copy = pltpu.make_async_copy(mine, out, wo_s.at[j])
        copy.start()
        outs.append(copy)

    back_landed(7, 0)
    for d in range(2):
        for s in range(PARTS):
            send(red_copy(d, 0, s))
    for d in range(2):
        back_landed(block(1 - d, 3), 0)
        for s in range(PARTS):
            send(red_copy(d, 1, s))
    prob_stage(1)
    grad_gate_up()
    send(wx_copy(0))
    send(wx_copy(1))
    for s in range(PARTS):
        for d in range(2):
            red_copy(d, 0, s).wait_recv()
            send(red_copy(d, 2, s))
    prob_stage(2)
    grad_down()
    send(wx_copy(2))
    for d in range(2):
        back_landed(block(1 - d, 2), 0)
    for s in range(PARTS):
        cols = slice(s * width, (s + 1) * width)
        for d in range(2):
            b = block(1 - d, 2)
            part = spread_rows(near_hot(gm[b]), yx[b, :, cols])
            red_copy(d, 1, s).wait_recv()
            red_copy(d, 2, s).wait_recv()
            part = part + spread_rows(far_hot(1 - d), f2[d, :, cols])
            sx[d, 0, :, cols] = part.astype(BF16)
            send(red_copy(d, 3, s))
    prob_stage(3)
    finish_weight(0)
    for j in range(2):
        metax_copy(j).wait_recv()
    for d in range(2):
        back_landed(block(1 - d, 1), 0)
    for s in range(PARTS):
        cols = slice(s * width, (s + 1) * width)
        for d in range(2):
            b = block(1 - d, 1)
            meta = gmx[1] if d == 0 else gm[b]
            part = spread_rows(near_hot(meta), yx[b, :, cols])
            red_copy(d, 3, s).wait_recv()
            sx[d, 1, :, cols] = (part + rx[d, 0, :, cols].astype(F32)).astype(BF16)
            send(red_copy(d, 4, s))
    prob_stage(4)
    finish_weight(1)
    finish_weight(2)
    back_landed(0, 0)
    back_landed(0, 1)
    for s in range(PARTS):
        cols = slice(s * width, (s + 1) * width)
        part = spread_rows(near_hot(gmx[0]), yx[0, :, cols])
        for d in range(2):
            red_copy(d, 4, s).wait_recv()
        part = part + rx[0, 1, :, cols].astype(F32) + rx[1, 1, :, cols].astype(F32)
        fin[:, cols] = part.astype(BF16)
        at = pl.ds(s * width, width)
        copy = pltpu.make_async_copy(fin.at[:, at], gi_out.at[:, at], fin_s.at[s])
        copy.start()
        outs.append(copy)
    for d in range(2):
        redp_copy(d, 4).wait_recv()
    pg_out[...] = (prob_part(0) + rpp[0, 3] + rpp[1, 3])[0:2, :]
    for copy in pending:
        copy.wait_send()
    for copy in outs:
        copy.wait()


def hand_over(gi, pg, og, ou, od, gi_out, pg_out, og_out, ou_out, od_out, b_gi, b_og, b_ou, b_od, in_sem, out_sem):
    pg_out[...] = pg[...]
    pieces = []
    for src, held, dst in ((gi, b_gi, gi_out), (og, b_og, og_out), (ou, b_ou, ou_out), (od, b_od, od_out)):
        step = max(src.shape[0] // 4, 128)
        for first in range(0, src.shape[0], step):
            rows = pl.ds(first, step)
            pieces.append((src.at[rows], held.at[rows], dst.at[rows]))
    loads = [pltpu.make_async_copy(p[0], p[1], in_sem.at[j]) for j, p in enumerate(pieces)]
    stores = [pltpu.make_async_copy(p[1], p[2], out_sem.at[j]) for j, p in enumerate(pieces)]
    for copy in loads:
        copy.start()
    for load, store in zip(loads, stores):
        load.wait()
        store.start()
    for copy in stores:
        copy.wait()


def per_device(tokens, out_grad, expert_ids, route_probs, gate_weight, up_weight, down_weight):
    rows, d_model = tokens.shape[1:]
    hid = gate_weight.shape[3]
    full = 2 * hid
    vmem = pltpu.VMEM
    dma = pltpu.SemaphoreType.DMA
    in_vmem = pl.BlockSpec(memory_space=pltpu.VMEM)
    anywhere = pl.BlockSpec(memory_space=pl.ANY)
    n_slots = NZ * SLOTS
    scratch = [
        vmem((4, ROWS, d_model), BF16), vmem((4, ROWS, d_model), BF16), vmem((8, 8, ROWS), F32), vmem((2, 8, ROWS), F32),
        vmem((8, SLOTS, d_model), BF16), vmem((8, SLOTS, d_model), BF16), vmem((8, SLOTS, ROWS), F32),
        vmem((2, 2, FAR, d_model), BF16), vmem((2, 2, FAR, d_model), BF16),
        vmem((n_slots, d_model), BF16), vmem((n_slots, d_model), BF16), vmem((n_slots, ROWS), F32),
        vmem((d_model, full), BF16), vmem((d_model, full), BF16), vmem((full, d_model), BF16),
        vmem((LAST, full), F32), vmem((LAST, full), F32),
        vmem((n_slots, full), BF16), vmem((n_slots, full), BF16), vmem((n_slots, full), BF16),
        vmem((n_slots, d_model), BF16), vmem((n_slots, ROWS), F32),
        vmem((8, SLOTS, d_model), BF16), vmem((8, SLOTS, ROWS), F32),
        vmem((2, HALF, d_model), BF16), vmem((2, FAR, d_model), BF16),
        vmem((2, 2, ROWS, d_model), BF16), vmem((2, 2, ROWS, d_model), BF16),
        vmem((2, 4, 8, ROWS), F32), vmem((2, 4, 8, ROWS), F32),
        vmem((ROWS, d_model), BF16),
        vmem((d_model, hid), BF16), vmem((d_model, hid), BF16), vmem((hid, d_model), BF16),
        vmem((d_model, hid), BF16), vmem((d_model, hid), BF16), vmem((hid, d_model), BF16),
        vmem((d_model, hid), BF16), vmem((d_model, hid), BF16), vmem((hid, d_model), BF16),
        dma((2, 2, 4)), dma((2, 2, 4)), dma((2, 4)), dma((2, 4)), dma((2,)), dma((2,)),
        dma((8, 3, 3)), dma((8, 3, 3)), dma((8, 4, 2)), dma((8, 4, 2)),
        dma((2, 5, PARTS)), dma((2, 5, PARTS)), dma((2, 4)), dma((2, 4)),
        dma((PARTS,)), dma((3,)), dma((3,)), dma((3,)), dma((3,)), dma((3,)), dma((3,)),
    ]
    shapes = (
        jax.ShapeDtypeStruct((rows, d_model), BF16), jax.ShapeDtypeStruct((2, rows), F32),
        jax.ShapeDtypeStruct((d_model, hid), BF16), jax.ShapeDtypeStruct((d_model, hid), BF16),
        jax.ShapeDtypeStruct((hid, d_model), BF16))
    results = pl.pallas_call(
        kernel,
        out_shape=shapes,
        in_specs=[in_vmem, in_vmem, in_vmem, in_vmem, anywhere, anywhere, anywhere],
        out_specs=(anywhere, in_vmem, anywhere, anywhere, anywhere),
        scratch_shapes=scratch,
        compiler_params=pltpu.CompilerParams(
            collective_id=0, has_side_effects=True, vmem_limit_bytes=62 * 1024 * 1024),
    )(expert_ids[0].T, route_probs[0].T, tokens[0], out_grad[0], gate_weight[0, 0], up_weight[0, 0], down_weight[0, 0])
    grad_in, prob, grad_gate, grad_up, grad_down = pl.pallas_call(
        hand_over,
        out_shape=shapes,
        in_specs=[anywhere, in_vmem, anywhere, anywhere, anywhere],
        out_specs=(anywhere, in_vmem, anywhere, anywhere, anywhere),
        scratch_shapes=[
            vmem((rows, d_model), BF16), vmem((d_model, hid), BF16), vmem((d_model, hid), BF16), vmem((hid, d_model), BF16),
            dma((16,)), dma((16,))],
    )(*results)
    return (
        grad_in[None], prob.T[None], grad_gate[None, None], grad_up[None, None], grad_down[None, None])


def solution(mesh):
    in_specs = (
        P("section", ("dp", "expert"), None), P("section", ("dp", "expert"), None),
        P("section", ("dp", "expert"), None), P("section", ("dp", "expert"), None),
        P("section", "expert", None, "dp"), P("section", "expert", None, "dp"), P("section", "expert", "dp", None))
    out_specs = (
        P("section", ("dp", "expert"), None), P("section", ("dp", "expert"), None),
        P("section", "expert", None, "dp"), P("section", "expert", None, "dp"), P("section", "expert", "dp", None))
    return jax.shard_map(per_device, mesh=mesh, in_specs=in_specs, out_specs=out_specs, check_vma=False)
```

time: 186 us -> 159 us (0.85)
  the two profiles are of different devices: /device:TPU:2 before, /device:TPU:60 now
where the time goes in v2:
time: 159 us
  Pallas kernels  159 us (100%)
    pallas_call x1, Pallas kernels, per_device(): pl.pallas_call(kernel, out_shape=shapes, in_specs=[in_vmem, in_vmem, in_v...  153 us
    pallas_call x1, Pallas kernels, per_device(): pl.pallas_call(hand_over, out_shape=shapes, in_specs=[anywhere, in_vmem,...  6.05 us

profile of v2, /device:TPU:60, one launch (start us, length us, event | category | flops | bytes accessed | tf_op | source)
XLA Modules:
  0.0 159.2 jit_solution(2722805561687632710)
XLA Ops:
  0.6 152.5 %shard_map.110 = (bf16[128,2048]{1,0:T(8,128)(2,1)}, f32[2,128]{1,0:T(2,128)}, bf16[2048,384]{1,0:T(8,128)(2,1)}, bf16[2048,384]{1,0:T(8,128)(2,1)}, bf16[384,2048]{1,0:T(8,128)(2,1)}) custom-call(s32[2,128]{1,0:T(2,128)} %bitcast.23, f32[2,128]{1,0:T(2,128)} %bitcast.24, bf16[128,2048]{1,0:T(8,128)(2,1)} %bitcast.21, bf16[128,2048]{1,0:T(8,128)(2,1)} %bitcast.22, ...), custom_call_target="tpu_custom_call" | custom-call | tf_op jit(solution)/shard_map/pallas_call | solution.py:532
  153.1 6.1 %shard_map.111 = (bf16[128,2048]{1,0:T(8,128)(2,1)}, f32[2,128]{1,0:T(2,128)}, bf16[2048,384]{1,0:T(8,128)(2,1)}, bf16[2048,384]{1,0:T(8,128)(2,1)}, bf16[384,2048]{1,0:T(8,128)(2,1)}) custom-call(bf16[128,2048]{1,0:T(8,128)(2,1)} %get-tuple-element.15.gi, f32[2,128]{1,0:T(2,128)} %get-tuple-element.16.pg, bf16[2048,384]{1,0:T(8,128)(2,1)} %get-tuple-element.17.og, ...), custom_call_target="tpu_custom_call" | custom-call | tf_op jit(solution)/shard_map/pallas_call | solution.py:541

commit v3 on v2

--- a/solution.py
+++ b/solution.py
@@ -33,15 +33,16 @@
 
 
 def kernel(
-    ids_ref, probs_ref, t_ref, g_ref, wg_hbm, wu_hbm, wd_hbm,
+    ids_ref, probs_ref, t_hbm, g_hbm, wg_hbm, wu_hbm, wd_hbm,
     gi_out, pg_out, og_out, ou_out, od_out,
-    gt, gg, gm, gmx, tp, gp, pp, fs, fr, rt, rg, rp, wg, wu, wd,
-    z_gate, z_up, a_gate, a_up, a_act, dx, pr, yx, yp, f1, f2, sx, rx, sp, rpp, fin,
-    wsg, wsu, wsd, wrg, wru, wrd, wog, wou, wod,
-    ring_s, ring_r, meta_s, meta_r, mx_s, mx_r, disp_s, disp_r, back_s, back_r,
-    red_s, red_r, redp_s, redp_r, fin_s, w_l, w_s, w_r, wx_s, wx_r, wo_s,
+    t_ref, g_ref, gt, gg, gm, gmx, tp, gp, pp, fs, fr, rt, rg, rp, wg, wu, wd,
+    wgt, wut, wdt,
+    z_gate, z_up, a_gate, a_up, a_act, dx, pr, yx, yp, f1, f2, sx, rx, sp, rpp,
+    wrg, wru, wrd,
+    ring_s, ring_r, meta_s, meta_r, mx_s, mx_r, disp_s, disp_r, back_s, back_r, part_s, part_r,
+    red_s, red_r, redp_s, redp_r, x_l, w_l, w_s, w_r, wx_s, wx_r,
 ):
-    d_model = t_ref.shape[1]
+    d_model = t_hbm.shape[1]
     hid = wg_hbm.shape[1]
     full = 2 * hid
     me = lax.axis_index("expert")
@@ -83,6 +84,34 @@
     for copy in local_w:
         copy.start()
 
+    local_x = [pltpu.make_async_copy(t_hbm, t_ref, x_l.at[0]), pltpu.make_async_copy(g_hbm, g_ref, x_l.at[1])]
+    for copy in local_x:
+        copy.start()
+
+    pl.semaphore_wait(barrier, len(greet))
+
+    def meta_copy(d, k):
+        src = gm.at[0] if k == 1 else gm.at[block(d, k - 1)]
+        return remote(src, gm.at[block(d, k)], meta_s.at[d, k - 1], meta_r.at[d, k - 1], ring_to[d])
+
+    def metax_copy(j):
+        return remote(gm.at[AHEAD[j]], gmx.at[j], mx_s.at[j], mx_r.at[j], {"section": x_prev})
+
+    def ring_copy(x, d, k):
+        own, held, staged = ((t_hbm, gt, tp), (g_hbm, gg, gp))[x]
+        if k == 1:
+            src, dst = own, held.at[block(d, 1) - 1]
+        elif k == 2:
+            src, dst = held.at[block(d, 1) - 1], held.at[block(d, 2) - 1]
+        elif k == 3:
+            src, dst = fs.at[x, d], fr.at[x, d]
+        else:
+            src, dst = fr.at[x, d, pl.ds(SLOTS, HALF)], staged.at[7, pl.ds(d * HALF, HALF)]
+        return remote(src, dst, ring_s.at[x, d, k - 1], ring_r.at[x, d, k - 1], ring_to[d])
+
+    for d in range(2):
+        send(ring_copy(0, d, 1))
+
     ids = ids_ref[...].astype(F32)
     experts = lax.broadcasted_iota(jnp.int32, (NY * NZ, ROWS), 0).astype(F32)
     hit0 = jnp.where(experts == ids[0:1, :], 1.0, 0.0)
@@ -95,32 +124,10 @@
     slot1 = ids[1:2, :] * CAP + jnp.sum(hit1 * before, axis=0, keepdims=True)
     gm[0] = jnp.concatenate([slot0, slot1, probs_ref[...], jnp.zeros((4, ROWS), F32)], axis=0)
 
-    pl.semaphore_wait(barrier, len(greet))
-
-    def meta_copy(d, k):
-        src = gm.at[0] if k == 1 else gm.at[block(d, k - 1)]
-        return remote(src, gm.at[block(d, k)], meta_s.at[d, k - 1], meta_r.at[d, k - 1], ring_to[d])
-
-    def metax_copy(j):
-        return remote(gm.at[AHEAD[j]], gmx.at[j], mx_s.at[j], mx_r.at[j], {"section": x_prev})
-
-    def ring_copy(x, d, k):
-        own, held, staged = ((t_ref, gt, tp), (g_ref, gg, gp))[x]
-        if k == 1:
-            src, dst = own, held.at[block(d, 1) - 1]
-        elif k == 2:
-            src, dst = held.at[block(d, 1) - 1], held.at[block(d, 2) - 1]
-        elif k == 3:
-            src, dst = fs.at[x, d], fr.at[x, d]
-        else:
-            src, dst = fr.at[x, d, pl.ds(SLOTS, HALF)], staged.at[7, pl.ds(d * HALF, HALF)]
-        return remote(src, dst, ring_s.at[x, d, k - 1], ring_r.at[x, d, k - 1], ring_to[d])
-
     for d in range(2):
         send(meta_copy(d, 1))
-    for x in range(2):
-        for d in range(2):
-            send(ring_copy(x, d, 1))
+    for d in range(2):
+        send(ring_copy(1, d, 1))
     send(metax_copy(0))
     w_copies = [
         remote(wg_hbm, wg.at[:, pl.ds(hid, hid)], w_s.at[0], w_r.at[0], twin),
@@ -206,7 +213,7 @@
             z_gate[0:count, cols] = jnp.dot(tok, wg[:, cols], preferred_element_type=F32)
             z_up[0:count, cols] = jnp.dot(tok, wu[:, cols], preferred_element_type=F32)
 
-    def hidden_dx(first, count):
+    def activations(first, count):
         tile = 256
         rows = pl.ds(first, count)
         pr[rows, :] = jnp.zeros((count, ROWS), F32)
@@ -214,7 +221,7 @@
         @pl.loop(0, full // tile)
         def _(n):
             cols = pl.ds(pl.multiple_of(n * tile, tile), tile)
-            hidden = lax.dot_general(rg[rows, :], wd[cols, :], NT, preferred_element_type=F32)
+            hidden = jnp.dot(rg[rows, :], wdt[:, cols], preferred_element_type=F32)
             gate = z_gate[0:count, cols]
             up = z_up[0:count, cols]
             prob = rp[rows, :][:, 0:1]
@@ -227,14 +234,20 @@
             a_gate[rows, cols] = (scaled * up * sig * (1.0 + gate * (1.0 - sig))).astype(BF16)
             a_up[rows, cols] = (scaled * silu).astype(BF16)
 
-        tile_d = 512
-
-        @pl.loop(0, d_model // tile_d)
-        def _(n):
-            cols = pl.ds(pl.multiple_of(n * tile_d, tile_d), tile_d)
-            out = lax.dot_general(a_gate[rows, :], wg[cols, :], NT, preferred_element_type=F32)
-            out += lax.dot_general(a_up[rows, :], wu[cols, :], NT, preferred_element_type=F32)
-            dx[rows, cols] = out.astype(BF16)
+    width = d_model // PARTS
+
+    def dx_part(first, count, part):
+        rows = pl.ds(first, count)
+        cols = pl.ds(part * width, width) if isinstance(part, int) else pl.ds(pl.multiple_of(part * width, width), width)
+        out = jnp.dot(a_gate[rows, :], wgt[:, cols], preferred_element_type=F32)
+        out += jnp.dot(a_up[rows, :], wut[:, cols], preferred_element_type=F32)
+        dx[rows, cols] = out.astype(BF16)
+
+    def part_copy(b, i, part):
+        cols = pl.ds(part * width, width)
+        return remote(
+            dx.at[pl.ds(b * SLOTS + (NY - i) * CAP, CAP), cols], yx.at[b, pl.ds(i * CAP, CAP), cols],
+            part_s.at[b - 5, i - 1, part], part_r.at[b - 5, i - 1, part], y_to[NY - i])
 
     def send_back(blocks):
         for b in blocks:
@@ -253,9 +266,16 @@
             for x in (0, 1, 2):
                 landed(b, x)
         gate_up(first, count)
-        hidden_dx(first, count)
+        activations(first, count)
+
+        @pl.loop(0, PARTS)
+        def _(part):
+            dx_part(first, count, part)
+
         send_back(blocks)
 
+    for copy in local_x:
+        copy.wait()
     for x in (2, 0, 1):
         pack(0, x)
     for d in range(2):
@@ -273,6 +293,18 @@
         copy.wait()
     for copy in w_copies:
         copy.wait_recv()
+
+    @pl.loop(0, full // 256)
+    def _(n):
+        at = pl.ds(pl.multiple_of(n * 256, 256), 256)
+        wdt[:, at] = wd[at, :].T
+
+    @pl.loop(0, d_model // 256)
+    def _(n):
+        at = pl.ds(pl.multiple_of(n * 256, 256), 256)
+        wgt[:, at] = wg[at, :].T
+        wut[:, at] = wu[at, :].T
+
     for d in range(2):
         meta_copy(d, 2).wait_recv()
         send(meta_copy(d, 3))
@@ -314,10 +346,19 @@
     for b in (5, 6, 7):
         landed(b, 1)
         landed(b, 2)
-    hidden_dx(5 * SLOTS, LAST)
-    send_back((7, 5, 6))
-
-    width = d_model // PARTS
+    activations(5 * SLOTS, LAST)
+    for b in (7, 5, 6):
+        for i in range(1, NY):
+            send(back_copy(b, i, 1))
+        yp[b, 0:CAP, :] = pr[b * SLOTS:b * SLOTS + CAP, :]
+    for part in range(PARTS):
+        dx_part(5 * SLOTS, LAST, part)
+        for b in (7, 5, 6):
+            for i in range(1, NY):
+                send(part_copy(b, i, part))
+        for b in (7, 5, 6):
+            top, cols = slice(b * SLOTS, b * SLOTS + CAP), slice(part * width, (part + 1) * width)
+            yx[b, 0:CAP, cols] = dx[top, cols]
 
     def red_copy(d, m, s):
         cols = pl.ds(s * width, width)
@@ -365,34 +406,33 @@
         return lax.dot_general(hot, rows, TN, preferred_element_type=F32)
 
     tile = 256
-
-    def grad_gate_up():
-        @pl.loop(0, d_model // tile)
+    pieces = d_model // tile // PARTS
+    out_half = ((wg.at[:, pl.ds(0, hid)], wrg, og_out), (wu.at[:, pl.ds(0, hid)], wru, ou_out), (wd.at[pl.ds(0, hid)], wrd, od_out))
+
+    def grad_gate_up(part):
+        @pl.loop(part * pieces, (part + 1) * pieces)
         def _(n):
             at = pl.ds(pl.multiple_of(n * tile, tile), tile)
             tok = rt[:, at]
-            for acts, other, mine in ((a_gate, wsg, wog), (a_up, wsu, wou)):
+            for acts, other, mine in ((a_gate, wg, og_out), (a_up, wu, ou_out)):
                 out = lax.dot_general(tok, acts[...], TN, preferred_element_type=F32).astype(BF16)
                 mine[at, :] = out[:, 0:hid]
-                other[at, :] = out[:, hid:full]
-
-    def grad_down():
-        @pl.loop(0, d_model // tile)
+                other[at, 0:hid] = out[:, hid:full]
+
+    def grad_down(part):
+        @pl.loop(part * pieces, (part + 1) * pieces)
         def _(n):
             at = pl.ds(pl.multiple_of(n * tile, tile), tile)
             out = lax.dot_general(a_act[...], rg[:, at], TN, preferred_element_type=F32).astype(BF16)
-            wod[:, at] = out[0:hid, :]
-            wsd[:, at] = out[hid:full, :]
-
-    trio = ((wsg, wrg, wog, og_out), (wsu, wru, wou, ou_out), (wsd, wrd, wod, od_out))
-    outs = []
+            od_out[:, at] = out[0:hid, :]
+            wd[0:hid, at] = out[hid:full, :]
 
     def wx_copy(j):
-        return remote(trio[j][0], trio[j][1], wx_s.at[j], wx_r.at[j], twin)
+        return remote(out_half[j][0], out_half[j][1], wx_s.at[j], wx_r.at[j], twin)
 
     def finish_weight(j):
         wx_copy(j).wait_recv()
-        _, got, mine, out = trio[j]
+        _, got, mine = out_half[j]
         step = mine.shape[0] // 4
 
         @pl.loop(0, 4)
@@ -400,29 +440,28 @@
             at = pl.ds(pl.multiple_of(n * step, step), step)
             mine[at, :] = (mine[at, :].astype(F32) + got[at, :].astype(F32)).astype(BF16)
 
-        copy = pltpu.make_async_copy(mine, out, wo_s.at[j])
-        copy.start()
-        outs.append(copy)
-
-    back_landed(7, 0)
-    for d in range(2):
-        for s in range(PARTS):
-            send(red_copy(d, 0, s))
-    for d in range(2):
-        back_landed(block(1 - d, 3), 0)
-        for s in range(PARTS):
-            send(red_copy(d, 1, s))
-    prob_stage(1)
-    grad_gate_up()
+    for s in range(PARTS):
+        for b in (7, 5, 6):
+            for i in range(1, NY):
+                part_copy(b, i, s).wait_recv()
+            if b == 7:
+                for d in range(2):
+                    send(red_copy(d, 0, s))
+            else:
+                send(red_copy(6 - b, 1, s))
+        if s in (1, 3):
+            prob_stage((s + 1) // 2)
+        if s > 0:
+            for d in range(2):
+                red_copy(d, 0, s - 1).wait_recv()
+                send(red_copy(d, 2, s - 1))
+        if s == PARTS - 1:
+            for d in range(2):
+                red_copy(d, 0, s).wait_recv()
+                send(red_copy(d, 2, s))
+        grad_gate_up(s)
     send(wx_copy(0))
     send(wx_copy(1))
-    for s in range(PARTS):
-        for d in range(2):
-            red_copy(d, 0, s).wait_recv()
-            send(red_copy(d, 2, s))
-    prob_stage(2)
-    grad_down()
-    send(wx_copy(2))
     for d in range(2):
         back_landed(block(1 - d, 2), 0)
     for s in range(PARTS):
@@ -435,8 +474,10 @@
             part = part + spread_rows(far_hot(1 - d), f2[d, :, cols])
             sx[d, 0, :, cols] = part.astype(BF16)
             send(red_copy(d, 3, s))
-    prob_stage(3)
-    finish_weight(0)
+        if s == 1:
+            prob_stage(3)
+        grad_down(s)
+    send(wx_copy(2))
     for j in range(2):
         metax_copy(j).wait_recv()
     for d in range(2):
@@ -450,9 +491,10 @@
             red_copy(d, 3, s).wait_recv()
             sx[d, 1, :, cols] = (part + rx[d, 0, :, cols].astype(F32)).astype(BF16)
             send(red_copy(d, 4, s))
-    prob_stage(4)
-    finish_weight(1)
-    finish_weight(2)
+        if s == 1:
+            prob_stage(4)
+        if s < 3:
+            finish_weight(s)
     back_landed(0, 0)
     back_landed(0, 1)
     for s in range(PARTS):
@@ -461,37 +503,12 @@
         for d in range(2):
             red_copy(d, 4, s).wait_recv()
         part = part + rx[0, 1, :, cols].astype(F32) + rx[1, 1, :, cols].astype(F32)
-        fin[:, cols] = part.astype(BF16)
-        at = pl.ds(s * width, width)
-        copy = pltpu.make_async_copy(fin.at[:, at], gi_out.at[:, at], fin_s.at[s])
-        copy.start()
-        outs.append(copy)
+        gi_out[:, cols] = part.astype(BF16)
     for d in range(2):
         redp_copy(d, 4).wait_recv()
     pg_out[...] = (prob_part(0) + rpp[0, 3] + rpp[1, 3])[0:2, :]
     for copy in pending:
         copy.wait_send()
-    for copy in outs:
-        copy.wait()
-
-
-def hand_over(gi, pg, og, ou, od, gi_out, pg_out, og_out, ou_out, od_out, b_gi, b_og, b_ou, b_od, in_sem, out_sem):
-    pg_out[...] = pg[...]
-    pieces = []
-    for src, held, dst in ((gi, b_gi, gi_out), (og, b_og, og_out), (ou, b_ou, ou_out), (od, b_od, od_out)):
-        step = max(src.shape[0] // 4, 128)
-        for first in range(0, src.shape[0], step):
-            rows = pl.ds(first, step)
-            pieces.append((src.at[rows], held.at[rows], dst.at[rows]))
-    loads = [pltpu.make_async_copy(p[0], p[1], in_sem.at[j]) for j, p in enumerate(pieces)]
-    stores = [pltpu.make_async_copy(p[1], p[2], out_sem.at[j]) for j, p in enumerate(pieces)]
-    for copy in loads:
-        copy.start()
-    for load, store in zip(loads, stores):
-        load.wait()
-        store.start()
-    for copy in stores:
-        copy.wait()
 
 
 def per_device(tokens, out_grad, expert_ids, route_probs, gate_weight, up_weight, down_weight):
@@ -504,11 +521,13 @@
     anywhere = pl.BlockSpec(memory_space=pl.ANY)
     n_slots = NZ * SLOTS
     scratch = [
+        vmem((rows, d_model), BF16), vmem((rows, d_model), BF16),
         vmem((4, ROWS, d_model), BF16), vmem((4, ROWS, d_model), BF16), vmem((8, 8, ROWS), F32), vmem((2, 8, ROWS), F32),
         vmem((8, SLOTS, d_model), BF16), vmem((8, SLOTS, d_model), BF16), vmem((8, SLOTS, ROWS), F32),
         vmem((2, 2, FAR, d_model), BF16), vmem((2, 2, FAR, d_model), BF16),
         vmem((n_slots, d_model), BF16), vmem((n_slots, d_model), BF16), vmem((n_slots, ROWS), F32),
         vmem((d_model, full), BF16), vmem((d_model, full), BF16), vmem((full, d_model), BF16),
+        vmem((full, d_model), BF16), vmem((full, d_model), BF16), vmem((d_model, full), BF16),
         vmem((LAST, full), F32), vmem((LAST, full), F32),
         vmem((n_slots, full), BF16), vmem((n_slots, full), BF16), vmem((n_slots, full), BF16),
         vmem((n_slots, d_model), BF16), vmem((n_slots, ROWS), F32),
@@ -516,37 +535,25 @@
         vmem((2, HALF, d_model), BF16), vmem((2, FAR, d_model), BF16),
         vmem((2, 2, ROWS, d_model), BF16), vmem((2, 2, ROWS, d_model), BF16),
         vmem((2, 4, 8, ROWS), F32), vmem((2, 4, 8, ROWS), F32),
-        vmem((ROWS, d_model), BF16),
-        vmem((d_model, hid), BF16), vmem((d_model, hid), BF16), vmem((hid, d_model), BF16),
-        vmem((d_model, hid), BF16), vmem((d_model, hid), BF16), vmem((hid, d_model), BF16),
         vmem((d_model, hid), BF16), vmem((d_model, hid), BF16), vmem((hid, d_model), BF16),
         dma((2, 2, 4)), dma((2, 2, 4)), dma((2, 4)), dma((2, 4)), dma((2,)), dma((2,)),
-        dma((8, 3, 3)), dma((8, 3, 3)), dma((8, 4, 2)), dma((8, 4, 2)),
+        dma((8, 3, 3)), dma((8, 3, 3)), dma((8, 4, 2)), dma((8, 4, 2)), dma((3, 3, PARTS)), dma((3, 3, PARTS)),
         dma((2, 5, PARTS)), dma((2, 5, PARTS)), dma((2, 4)), dma((2, 4)),
-        dma((PARTS,)), dma((3,)), dma((3,)), dma((3,)), dma((3,)), dma((3,)), dma((3,)),
+        dma((2,)), dma((3,)), dma((3,)), dma((3,)), dma((3,)), dma((3,)),
     ]
     shapes = (
         jax.ShapeDtypeStruct((rows, d_model), BF16), jax.ShapeDtypeStruct((2, rows), F32),
         jax.ShapeDtypeStruct((d_model, hid), BF16), jax.ShapeDtypeStruct((d_model, hid), BF16),
         jax.ShapeDtypeStruct((hid, d_model), BF16))
-    results = pl.pallas_call(
+    grad_in, prob, grad_gate, grad_up, grad_down = pl.pallas_call(
         kernel,
-        out_shape=shapes,
-        in_specs=[in_vmem, in_vmem, in_vmem, in_vmem, anywhere, anywhere, anywhere],
-        out_specs=(anywhere, in_vmem, anywhere, anywhere, anywhere),
+        out_shape=tuple(vmem(shape.shape, shape.dtype) for shape in shapes),
+        in_specs=[in_vmem, in_vmem] + [anywhere] * 5,
+        out_specs=(in_vmem,) * 5,
         scratch_shapes=scratch,
         compiler_params=pltpu.CompilerParams(
-            collective_id=0, has_side_effects=True, vmem_limit_bytes=62 * 1024 * 1024),
+            collective_id=0, has_side_effects=True, vmem_limit_bytes=57 * 1024 * 1024),
     )(expert_ids[0].T, route_probs[0].T, tokens[0], out_grad[0], gate_weight[0, 0], up_weight[0, 0], down_weight[0, 0])
-    grad_in, prob, grad_gate, grad_up, grad_down = pl.pallas_call(
-        hand_over,
-        out_shape=shapes,
-        in_specs=[anywhere, in_vmem, anywhere, anywhere, anywhere],
-        out_specs=(anywhere, in_vmem, anywhere, anywhere, anywhere),
-        scratch_shapes=[
-            vmem((rows, d_model), BF16), vmem((d_model, hid), BF16), vmem((d_model, hid), BF16), vmem((hid, d_model), BF16),
-            dma((16,)), dma((16,))],
-    )(*results)
     return (
         grad_in[None], prob.T[None], grad_gate[None, None], grad_up[None, None], grad_down[None, None])
 

time: 159 us -> 147 us (0.925)
  the two profiles are of different devices: /device:TPU:60 before, /device:TPU:2 now
where the time goes in v3:
time: 147 us
  Pallas kernels  141 us (96%)
  local copies, waits for them, and re-layouts  4.78 us (3%)
    pallas_call x1, Pallas kernels, per_device(): pl.pallas_call(kernel, out_shape=tuple((vmem(shape.shape, shape.dtype) fo...  141 us
    unnamed x5, local copies, waits for them, and re-layouts  4.78 us

profile of v3, /device:TPU:2, one launch (start us, length us, event | category | flops | bytes accessed | tf_op | source)
XLA Modules:
  0.0 146.6 jit_solution(8856150531543413818)
XLA Ops:
  0.6 141.2 %shard_map.110 = (bf16[128,2048]{1,0:T(8,128)(2,1)S(1)}, f32[2,128]{1,0:T(2,128)S(1)}, bf16[2048,384]{1,0:T(8,128)(2,1)S(1)}, bf16[2048,384]{1,0:T(8,128)(2,1)S(1)}, bf16[384,2048]{1,0:T(8,128)(2,1)S(1)}) custom-call(s32[2,128]{1,0:T(2,128)} %bitcast.28, f32[2,128]{1,0:T(2,128)} %bitcast.29, bf16[128,2048]{1,0:T(8,128)(2,1)} %bitcast.26, ...), custom_call_target="tpu_custom_call" | custom-call | tf_op jit(solution)/shard_map/pallas_call | solution.py:548
  141.8 0.8 copy.17
  142.6 0.6 copy.18
  143.2 1.1 copy.19
  144.3 1.1 copy.20
  145.5 1.1 copy.21

commit v4 on v3

--- a/solution.py
+++ b/solution.py
@@ -37,9 +37,9 @@
     gi_out, pg_out, og_out, ou_out, od_out,
     t_ref, g_ref, gt, gg, gm, gmx, tp, gp, pp, fs, fr, rt, rg, rp, wg, wu, wd,
     wgt, wut, wdt,
-    z_gate, z_up, a_gate, a_up, a_act, dx, pr, yx, yp, f1, f2, sx, rx, sp, rpp,
+    z_gate, z_up, a_gate, a_up, a_act, dx, pr, yx, yp, f2, sx, rx, sp, rpp,
     wrg, wru, wrd,
-    ring_s, ring_r, meta_s, meta_r, mx_s, mx_r, disp_s, disp_r, back_s, back_r, part_s, part_r,
+    ring_s, ring_r, near_s, near_r, half_s, half_r, meta_s, meta_r, mx_s, mx_r, disp_s, disp_r, back_s, back_r, part_s, part_r,
     red_s, red_r, redp_s, redp_r, x_l, w_l, w_s, w_r, wx_s, wx_r,
 ):
     d_model = t_hbm.shape[1]
@@ -56,6 +56,7 @@
     ring = (lax.rem(z + 1, NZ) * NY + y, lax.rem(z + NZ - 1, NZ) * NY + y)
     column = [z * NY + lax.rem(y + i, NY) for i in range(NY)]
     ring_to = [{"expert": e} for e in ring]
+    ring_two = [{"expert": lax.rem(z + 2, NZ) * NY + y}, {"expert": lax.rem(z + NZ - 2, NZ) * NY + y}]
     ring_x = [{"section": x_prev, "expert": e} for e in ring]
     y_to = [{"expert": e} for e in column]
     y_x = [{"section": x_prev, "expert": e} for e in column]
@@ -71,7 +72,7 @@
         pending.append(copy)
 
     barrier = pltpu.get_barrier_semaphore()
-    greet = ring_to + y_to[1:] + [twin] + y_x + ring_x
+    greet = ring_to + ring_two + y_to[1:] + [twin] + y_x + ring_x
     greet += [{"section": x_next, "expert": e} for e in column + list(ring)]
     for dev in greet:
         pl.semaphore_signal(barrier, inc=1, device_id=dev, device_id_type=MESH)
@@ -103,11 +104,18 @@
             src, dst = own, held.at[block(d, 1) - 1]
         elif k == 2:
             src, dst = held.at[block(d, 1) - 1], held.at[block(d, 2) - 1]
-        elif k == 3:
-            src, dst = fs.at[x, d], fr.at[x, d]
         else:
-            src, dst = fr.at[x, d, pl.ds(SLOTS, HALF)], staged.at[7, pl.ds(d * HALF, HALF)]
-        return remote(src, dst, ring_s.at[x, d, k - 1], ring_r.at[x, d, k - 1], ring_to[d])
+            src, dst = fs.at[x, d, pl.ds(SLOTS, HALF)], staged.at[7, pl.ds(d * HALF, HALF)]
+        return remote(
+            src, dst, ring_s.at[x, d, k - 1], ring_r.at[x, d, k - 1], ring_two[d] if k == 3 else ring_to[d])
+
+    half_width = d_model // 2
+
+    def near_copy(x, d, h):
+        cols = pl.ds(h * half_width, half_width)
+        return remote(
+            fs.at[x, d, pl.ds(0, SLOTS), cols], fr.at[x, d, pl.ds(0, SLOTS), cols],
+            near_s.at[x, d, h], near_r.at[x, d, h], ring_to[d])
 
     for d in range(2):
         send(ring_copy(0, d, 1))
@@ -189,9 +197,27 @@
         if x < 2 and b >= 5:
             (rt, rg)[x][top, :] = staged_at(b, x)[0:CAP, :]
 
+    def half_copy(b, i, h):
+        cols = pl.ds(h * half_width, half_width)
+        return remote(
+            fr.at[1, b - 5, pl.ds(i * CAP, CAP), cols], rg.at[pl.ds(b * SLOTS + (NY - i) * CAP, CAP), cols],
+            half_s.at[b - 5, i - 1, h], half_r.at[b - 5, i - 1, h], y_to[i])
+
+    def pack_half(d, h):
+        near_copy(1, d, h).wait_recv()
+        b = block(d, 3)
+        for i in range(1, NY):
+            send(half_copy(b, i, h))
+        cols = slice(h * half_width, (h + 1) * half_width)
+        rg[b * SLOTS:b * SLOTS + CAP, cols] = fr[1, d, 0:CAP, cols]
+
     def landed(b, x):
         for i in range(1, NY):
-            disp_copy(b, i, x).wait_recv()
+            if x == 1 and b in (5, 6):
+                for h in range(2):
+                    half_copy(b, i, h).wait_recv()
+            else:
+                disp_copy(b, i, x).wait_recv()
 
     def back_copy(b, i, x):
         rows = pl.ds(b * SLOTS + (0 if i == 0 else NY - i) * CAP, CAP)
@@ -314,6 +340,8 @@
             held = (gt, gg)[x]
             fs[x, d] = jnp.dot(far_hot(d), held[block(d, 2) - 1], preferred_element_type=F32).astype(BF16)
             send(ring_copy(x, d, 3))
+            for h in range(2):
+                send(near_copy(x, d, h))
         for d in range(2):
             if x == 0:
                 pack(block(d, 2), 2)
@@ -324,25 +352,28 @@
         meta_copy(d, 3).wait_recv()
         if d == 0:
             send(meta_copy(d, 4))
-    for x in range(2):
-        for d in range(2):
-            ring_copy(x, d, 3).wait_recv()
-            send(ring_copy(x, d, 4))
-        for d in range(2):
-            pack(block(d, 3), x)
-        if x == 0:
-            for d in range(2):
-                pack(block(d, 3), 2)
-            chunk((3, 4))
+    for d in range(2):
+        for h in range(2):
+            near_copy(0, d, h).wait_recv()
+        pack(block(d, 3), 0)
+    for d in range(2):
+        ring_copy(0, d, 3).wait_recv()
+    pack(7, 0)
+    for d in range(2):
+        pack(block(d, 3), 2)
+    chunk((3, 4))
     meta_copy(0, 4).wait_recv()
     pack(7, 2)
-    for x in range(2):
-        for d in range(2):
-            ring_copy(x, d, 4).wait_recv()
-        pack(7, x)
+    for d in range(2):
+        ring_copy(1, d, 3).wait_recv()
+    pack(7, 1)
+    for d in range(2):
+        pack_half(d, 0)
     for b in (5, 6, 7):
         landed(b, 0)
     gate_up(5 * SLOTS, LAST)
+    for d in range(2):
+        pack_half(d, 1)
     for b in (5, 6, 7):
         landed(b, 1)
         landed(b, 2)
@@ -364,11 +395,10 @@
         cols = pl.ds(s * width, width)
         dev = ring_to[d]
         if m == 0:
-            src, dst = yx.at[7, pl.ds((1 - d) * HALF, HALF), cols], f1.at[d, :, cols]
+            src, dst = yx.at[7, pl.ds((1 - d) * HALF, HALF), cols], f2.at[d, pl.ds(SLOTS, HALF), cols]
+            dev = ring_two[d]
         elif m == 1:
             src, dst = yx.at[block(1 - d, 3), :, cols], f2.at[d, pl.ds(0, SLOTS), cols]
-        elif m == 2:
-            src, dst = f1.at[d, :, cols], f2.at[d, pl.ds(SLOTS, HALF), cols]
         else:
             src, dst = sx.at[d, m - 3, :, cols], rx.at[d, m - 3, :, cols]
             if m == 3 + d:
@@ -451,14 +481,6 @@
                 send(red_copy(6 - b, 1, s))
         if s in (1, 3):
             prob_stage((s + 1) // 2)
-        if s > 0:
-            for d in range(2):
-                red_copy(d, 0, s - 1).wait_recv()
-                send(red_copy(d, 2, s - 1))
-        if s == PARTS - 1:
-            for d in range(2):
-                red_copy(d, 0, s).wait_recv()
-                send(red_copy(d, 2, s))
         grad_gate_up(s)
     send(wx_copy(0))
     send(wx_copy(1))
@@ -470,7 +492,7 @@
             b = block(1 - d, 2)
             part = spread_rows(near_hot(gm[b]), yx[b, :, cols])
             red_copy(d, 1, s).wait_recv()
-            red_copy(d, 2, s).wait_recv()
+            red_copy(d, 0, s).wait_recv()
             part = part + spread_rows(far_hot(1 - d), f2[d, :, cols])
             sx[d, 0, :, cols] = part.astype(BF16)
             send(red_copy(d, 3, s))
@@ -511,6 +533,15 @@
         copy.wait_send()
 
 
+def hand_over(gi, pg, og, ou, od, gi_out, pg_out, og_out, ou_out, od_out, sems):
+    pairs = ((og, og_out), (ou, ou_out), (od, od_out), (gi, gi_out), (pg, pg_out))
+    copies = [pltpu.make_async_copy(src, dst, sems.at[j]) for j, (src, dst) in enumerate(pairs)]
+    for copy in copies:
+        copy.start()
+    for copy in copies:
+        copy.wait()
+
+
 def per_device(tokens, out_grad, expert_ids, route_probs, gate_weight, up_weight, down_weight):
     rows, d_model = tokens.shape[1:]
     hid = gate_weight.shape[3]
@@ -524,7 +555,7 @@
         vmem((rows, d_model), BF16), vmem((rows, d_model), BF16),
         vmem((4, ROWS, d_model), BF16), vmem((4, ROWS, d_model), BF16), vmem((8, 8, ROWS), F32), vmem((2, 8, ROWS), F32),
         vmem((8, SLOTS, d_model), BF16), vmem((8, SLOTS, d_model), BF16), vmem((8, SLOTS, ROWS), F32),
-        vmem((2, 2, FAR, d_model), BF16), vmem((2, 2, FAR, d_model), BF16),
+        vmem((2, 2, FAR, d_model), BF16), vmem((2, 2, SLOTS, d_model), BF16),
         vmem((n_slots, d_model), BF16), vmem((n_slots, d_model), BF16), vmem((n_slots, ROWS), F32),
         vmem((d_model, full), BF16), vmem((d_model, full), BF16), vmem((full, d_model), BF16),
         vmem((full, d_model), BF16), vmem((full, d_model), BF16), vmem((d_model, full), BF16),
@@ -532,11 +563,12 @@
         vmem((n_slots, full), BF16), vmem((n_slots, full), BF16), vmem((n_slots, full), BF16),
         vmem((n_slots, d_model), BF16), vmem((n_slots, ROWS), F32),
         vmem((8, SLOTS, d_model), BF16), vmem((8, SLOTS, ROWS), F32),
-        vmem((2, HALF, d_model), BF16), vmem((2, FAR, d_model), BF16),
+        vmem((2, FAR, d_model), BF16),
         vmem((2, 2, ROWS, d_model), BF16), vmem((2, 2, ROWS, d_model), BF16),
         vmem((2, 4, 8, ROWS), F32), vmem((2, 4, 8, ROWS), F32),
         vmem((d_model, hid), BF16), vmem((d_model, hid), BF16), vmem((hid, d_model), BF16),
-        dma((2, 2, 4)), dma((2, 2, 4)), dma((2, 4)), dma((2, 4)), dma((2,)), dma((2,)),
+        dma((2, 2, 3)), dma((2, 2, 3)), dma((2, 2, 2)), dma((2, 2, 2)), dma((2, 3, 2)), dma((2, 3, 2)),
+        dma((2, 4)), dma((2, 4)), dma((2,)), dma((2,)),
         dma((8, 3, 3)), dma((8, 3, 3)), dma((8, 4, 2)), dma((8, 4, 2)), dma((3, 3, PARTS)), dma((3, 3, PARTS)),
         dma((2, 5, PARTS)), dma((2, 5, PARTS)), dma((2, 4)), dma((2, 4)),
         dma((2,)), dma((3,)), dma((3,)), dma((3,)), dma((3,)), dma((3,)),
@@ -545,7 +577,7 @@
         jax.ShapeDtypeStruct((rows, d_model), BF16), jax.ShapeDtypeStruct((2, rows), F32),
         jax.ShapeDtypeStruct((d_model, hid), BF16), jax.ShapeDtypeStruct((d_model, hid), BF16),
         jax.ShapeDtypeStruct((hid, d_model), BF16))
-    grad_in, prob, grad_gate, grad_up, grad_down = pl.pallas_call(
+    results = pl.pallas_call(
         kernel,
         out_shape=tuple(vmem(shape.shape, shape.dtype) for shape in shapes),
         in_specs=[in_vmem, in_vmem] + [anywhere] * 5,
@@ -554,6 +586,14 @@
         compiler_params=pltpu.CompilerParams(
             collective_id=0, has_side_effects=True, vmem_limit_bytes=57 * 1024 * 1024),
     )(expert_ids[0].T, route_probs[0].T, tokens[0], out_grad[0], gate_weight[0, 0], up_weight[0, 0], down_weight[0, 0])
+    grad_in, prob, grad_gate, grad_up, grad_down = pl.pallas_call(
+        hand_over,
+        out_shape=shapes,
+        in_specs=[in_vmem] * 5,
+        out_specs=(anywhere,) * 5,
+        scratch_shapes=[dma((5,))],
+        compiler_params=pltpu.CompilerParams(vmem_limit_bytes=1024 * 1024),
+    )(*[pltpu.with_memory_space_constraint(result, pltpu.VMEM) for result in results])
     return (
         grad_in[None], prob.T[None], grad_gate[None, None], grad_up[None, None], grad_down[None, None])
 

time: 147 us -> 142 us (0.966)
  local copies, waits for them, and re-layouts: 4.78 us -> 0 us
    unnamed x5 -> x0, local copies, waits for them, and re-layouts: 4.78 us -> none
    pallas_call x1, Pallas kernels: 141 us -> 139 us  [per_device(): pl.pallas_call(kernel, out_shape=tuple((vmem(shape.shape, shape.dtype) fo...]
    pallas_call x0 -> x1, Pallas kernels: none -> 2.39 us  [per_device(): pl.pallas_call(hand_over, out_shape=shapes, in_specs=[in_vmem] * 5, out_s...]
where the time goes in v4:
time: 142 us
  Pallas kernels  141 us (99%)
    pallas_call x1, Pallas kernels, per_device(): pl.pallas_call(kernel, out_shape=tuple((vmem(shape.shape, shape.dtype) fo...  139 us

profile of v4, /device:TPU:2, one launch (start us, length us, event | category | flops | bytes accessed | tf_op | source)
XLA Modules:
  0.0 141.7 jit_solution(1621316832040995291)
XLA Ops:
  0.6 138.7 %shard_map.110 = (bf16[128,2048]{1,0:T(8,128)(2,1)S(1)}, f32[2,128]{1,0:T(2,128)S(1)}, bf16[2048,384]{1,0:T(8,128)(2,1)S(1)}, bf16[2048,384]{1,0:T(8,128)(2,1)S(1)}, bf16[384,2048]{1,0:T(8,128)(2,1)S(1)}) custom-call(s32[2,128]{1,0:T(2,128)} %bitcast.23, f32[2,128]{1,0:T(2,128)} %bitcast.24, bf16[128,2048]{1,0:T(8,128)(2,1)} %bitcast.21, ...), custom_call_target="tpu_custom_call" | custom-call | tf_op jit(solution)/shard_map/pallas_call | solution.py:580
  139.3 2.4 %shard_map.111 = (bf16[128,2048]{1,0:T(8,128)(2,1)}, f32[2,128]{1,0:T(2,128)}, bf16[2048,384]{1,0:T(8,128)(2,1)}, bf16[2048,384]{1,0:T(8,128)(2,1)}, bf16[384,2048]{1,0:T(8,128)(2,1)}) custom-call(bf16[128,2048]{1,0:T(8,128)(2,1)S(1)} %get-tuple-element.15.gi, f32[2,128]{1,0:T(2,128)S(1)} %get-tuple-element.16.pg, ...), custom_call_target="tpu_custom_call" | custom-call | tf_op jit(solution)/shard_map/pallas_call | solution.py:589

commit v5 on v4

--- a/solution.py
+++ b/solution.py
@@ -58,6 +58,8 @@
     ring_to = [{"expert": e} for e in ring]
     ring_two = [{"expert": lax.rem(z + 2, NZ) * NY + y}, {"expert": lax.rem(z + NZ - 2, NZ) * NY + y}]
     ring_x = [{"section": x_prev, "expert": e} for e in ring]
+    planes = [[lax.rem(z + h, NZ), lax.rem(z + NZ - h, NZ)] for h in range(3)]
+    aslant = [[[{"expert": planes[h][d] * NY + lax.rem(y + i, NY)} for i in range(NY)] for d in range(2)] for h in range(3)]
     y_to = [{"expert": e} for e in column]
     y_x = [{"section": x_prev, "expert": e} for e in column]
     twin = {"dp": 1 - core}
@@ -72,7 +74,7 @@
         pending.append(copy)
 
     barrier = pltpu.get_barrier_semaphore()
-    greet = ring_to + ring_two + y_to[1:] + [twin] + y_x + ring_x
+    greet = aslant[1][0] + aslant[1][1] + aslant[2][0] + aslant[2][1] + y_to[1:] + [twin] + y_x + ring_x
     greet += [{"section": x_next, "expert": e} for e in column + list(ring)]
     for dev in greet:
         pl.semaphore_signal(barrier, inc=1, device_id=dev, device_id_type=MESH)
@@ -271,9 +273,11 @@
 
     def part_copy(b, i, part):
         cols = pl.ds(part * width, width)
+        q = (NY - i) % NY
+        d, hops, row = (1 - i // 2, 2, NY + i % 2) if b == 7 else (6 - b, 1, i)
         return remote(
-            dx.at[pl.ds(b * SLOTS + (NY - i) * CAP, CAP), cols], yx.at[b, pl.ds(i * CAP, CAP), cols],
-            part_s.at[b - 5, i - 1, part], part_r.at[b - 5, i - 1, part], y_to[NY - i])
+            dx.at[pl.ds(b * SLOTS + q * CAP, CAP), cols], f2.at[d, pl.ds(row * CAP, CAP), cols],
+            part_s.at[b - 5, i, part], part_r.at[b - 5, i, part], aslant[hops][d][q])
 
     def send_back(blocks):
         for b in blocks:
@@ -385,25 +389,16 @@
     for part in range(PARTS):
         dx_part(5 * SLOTS, LAST, part)
         for b in (7, 5, 6):
-            for i in range(1, NY):
+            for i in range(NY):
                 send(part_copy(b, i, part))
-        for b in (7, 5, 6):
-            top, cols = slice(b * SLOTS, b * SLOTS + CAP), slice(part * width, (part + 1) * width)
-            yx[b, 0:CAP, cols] = dx[top, cols]
 
     def red_copy(d, m, s):
         cols = pl.ds(s * width, width)
         dev = ring_to[d]
-        if m == 0:
-            src, dst = yx.at[7, pl.ds((1 - d) * HALF, HALF), cols], f2.at[d, pl.ds(SLOTS, HALF), cols]
-            dev = ring_two[d]
-        elif m == 1:
-            src, dst = yx.at[block(1 - d, 3), :, cols], f2.at[d, pl.ds(0, SLOTS), cols]
-        else:
-            src, dst = sx.at[d, m - 3, :, cols], rx.at[d, m - 3, :, cols]
-            if m == 3 + d:
-                dev = ring_x[d]
-        return remote(src, dst, red_s.at[d, m, s], red_r.at[d, m, s], dev)
+        src, dst = sx.at[d, m - 3, :, cols], rx.at[d, m - 3, :, cols]
+        if m == 3 + d:
+            dev = ring_x[d]
+        return remote(src, dst, red_s.at[d, m - 3, s], red_r.at[d, m - 3, s], dev)
 
     def redp_copy(d, m):
         return remote(sp.at[d, m - 1], rpp.at[d, m - 1], redp_s.at[d, m - 1], redp_r.at[d, m - 1], ring_to[d])
@@ -471,17 +466,9 @@
             mine[at, :] = (mine[at, :].astype(F32) + got[at, :].astype(F32)).astype(BF16)
 
     for s in range(PARTS):
-        for b in (7, 5, 6):
-            for i in range(1, NY):
-                part_copy(b, i, s).wait_recv()
-            if b == 7:
-                for d in range(2):
-                    send(red_copy(d, 0, s))
-            else:
-                send(red_copy(6 - b, 1, s))
-        if s in (1, 3):
-            prob_stage((s + 1) // 2)
         grad_gate_up(s)
+        if s == 2:
+            prob_stage(1)
     send(wx_copy(0))
     send(wx_copy(1))
     for d in range(2):
@@ -491,13 +478,15 @@
         for d in range(2):
             b = block(1 - d, 2)
             part = spread_rows(near_hot(gm[b]), yx[b, :, cols])
-            red_copy(d, 1, s).wait_recv()
-            red_copy(d, 0, s).wait_recv()
+            for c in range(NY):
+                part_copy(6 - d, c, s).wait_recv()
+            for c in (2 - 2 * d, 3 - 2 * d):
+                part_copy(7, c, s).wait_recv()
             part = part + spread_rows(far_hot(1 - d), f2[d, :, cols])
             sx[d, 0, :, cols] = part.astype(BF16)
             send(red_copy(d, 3, s))
-        if s == 1:
-            prob_stage(3)
+        if s == 3:
+            prob_stage(2)
         grad_down(s)
     send(wx_copy(2))
     for j in range(2):
@@ -513,8 +502,8 @@
             red_copy(d, 3, s).wait_recv()
             sx[d, 1, :, cols] = (part + rx[d, 0, :, cols].astype(F32)).astype(BF16)
             send(red_copy(d, 4, s))
-        if s == 1:
-            prob_stage(4)
+        if s in (2, 3):
+            prob_stage(1 + s)
         if s < 3:
             finish_weight(s)
     back_landed(0, 0)
@@ -569,8 +558,8 @@
         vmem((d_model, hid), BF16), vmem((d_model, hid), BF16), vmem((hid, d_model), BF16),
         dma((2, 2, 3)), dma((2, 2, 3)), dma((2, 2, 2)), dma((2, 2, 2)), dma((2, 3, 2)), dma((2, 3, 2)),
         dma((2, 4)), dma((2, 4)), dma((2,)), dma((2,)),
-        dma((8, 3, 3)), dma((8, 3, 3)), dma((8, 4, 2)), dma((8, 4, 2)), dma((3, 3, PARTS)), dma((3, 3, PARTS)),
-        dma((2, 5, PARTS)), dma((2, 5, PARTS)), dma((2, 4)), dma((2, 4)),
+        dma((8, 3, 3)), dma((8, 3, 3)), dma((8, 4, 2)), dma((8, 4, 2)), dma((3, NY, PARTS)), dma((3, NY, PARTS)),
+        dma((2, 2, PARTS)), dma((2, 2, PARTS)), dma((2, 4)), dma((2, 4)),
         dma((2,)), dma((3,)), dma((3,)), dma((3,)), dma((3,)), dma((3,)),
     ]
     shapes = (

time: 142 us -> 139 us (0.979)
  Pallas kernels: 141 us -> 138 us
    pallas_call x1, Pallas kernels: 139 us -> 136 us  [per_device(): pl.pallas_call(kernel, out_shape=tuple((vmem(shape.shape, shape.dtype) fo...]
where the time goes in v5:
time: 139 us
  Pallas kernels  138 us (99%)
    pallas_call x1, Pallas kernels, per_device(): pl.pallas_call(kernel, out_shape=tuple((vmem(shape.shape, shape.dtype) fo...  136 us

profile of v5, /device:TPU:2, one launch (start us, length us, event | category | flops | bytes accessed | tf_op | source)
XLA Modules:
  0.0 138.7 jit_solution(11118613192074163762)
XLA Ops:
  0.6 135.7 %shard_map.110 = (bf16[128,2048]{1,0:T(8,128)(2,1)S(1)}, f32[2,128]{1,0:T(2,128)S(1)}, bf16[2048,384]{1,0:T(8,128)(2,1)S(1)}, bf16[2048,384]{1,0:T(8,128)(2,1)S(1)}, bf16[384,2048]{1,0:T(8,128)(2,1)S(1)}) custom-call(s32[2,128]{1,0:T(2,128)} %bitcast.23, f32[2,128]{1,0:T(2,128)} %bitcast.24, bf16[128,2048]{1,0:T(8,128)(2,1)} %bitcast.21, ...), custom_call_target="tpu_custom_call" | custom-call | tf_op jit(solution)/shard_map/pallas_call | solution.py:569
  136.3 2.4 %shard_map.111 = (bf16[128,2048]{1,0:T(8,128)(2,1)}, f32[2,128]{1,0:T(2,128)}, bf16[2048,384]{1,0:T(8,128)(2,1)}, bf16[2048,384]{1,0:T(8,128)(2,1)}, bf16[384,2048]{1,0:T(8,128)(2,1)}) custom-call(bf16[128,2048]{1,0:T(8,128)(2,1)S(1)} %get-tuple-element.15.gi, f32[2,128]{1,0:T(2,128)S(1)} %get-tuple-element.16.pg, ...), custom_call_target="tpu_custom_call" | custom-call | tf_op jit(solution)/shard_map/pallas_call | solution.py:578
